TPU v7x, 128 devices: a whole 4x4x4 slice. The times are simulated.
128 devices in a mesh: off: 4 (over z_hi, core), img: 32 (over x, y, z_lo).
Axes of the slice: x: 4, y: 4, z: 4 (z_hi: 2, z_lo: 2; z = z_hi * 2 + z_lo), core: 2. Of those that a mesh axis runs over, the one named last changes fastest.
Arguments:
- shot_traces: bfloat16 [4, 32, 32, 4096], P('off', None, 'img'), may hold values from -6 to 6
- assign: int32 [32, 32, 4], P('off', 'img'), may hold values from 0 to 3, each once within a row
- aperture: int32 [32, 32], P('off', 'img'), may hold values from 0 to 1
- band: int32 [32, 1024], P('off', 'img'), may hold values from 0 to 3584
- interp: bfloat16 [1024, 512, 64], P('img'), may hold values from -0.25 to 0.25
- amp: bfloat16 [1024, 128, 128], P('img'), may hold values from -0.5 to 0.5
Outputs:
- image: float32 [64, 131072], P('off', 'img')
All inputs are finite; a program needn't handle non-finite values.
Results may differ from a plain program's by a relative error of at most 0.0065.
Values may be sent and summed in bfloat16 or wider, within the bound.
No kernel may reach another device: no remote copies, remote signals or barrier semaphores. Data moves between devices by JAX's collectives and lax.ppermute only.
A program may use at most 128 MiB of HBM per device.

v0:
```python
import functools
import math

import jax
import jax.numpy as jnp
from jax import lax
from jax.experimental import pallas as pl
from jax.experimental.pallas import tpu as pltpu
from jax.sharding import Mesh, PartitionSpec as P

LANES = 128
SUB = 8
OFF = ("zh", "core")
PLANE = ("x", "y")
IMG = ("x", "y", "zl")
EVERY = OFF + IMG
CODE_SHIFT = 7
TURNS = 8
MASK = jnp.int16


def in_vmem(array):
    return pltpu.with_memory_space_constraint(array, pltpu.VMEM)


def prepare_kernel(off_ref, assign_ref, band_ref, aperture_ref, traces_ref, out_ref, meta_ref, rows_ref, *, offs, pitch):
    blocks, samples = traces_ref.shape
    chunks = samples // LANES
    lane = lax.broadcasted_iota(jnp.int32, (blocks, LANES), 1)
    before = jnp.zeros((blocks, LANES), jnp.float32)
    for chunk in range(chunks):
        here = traces_ref[:, chunk * LANES : (chunk + 1) * LANES].astype(jnp.float32)
        turned = pltpu.roll(here, 1, 1)
        rows_ref[pl.ds(chunk, blocks, stride=chunks), :] = here - 0.9 * jnp.where(lane == 0, before, turned)
        before = turned
    for block in range(blocks):
        out_ref[block] = rows_ref[block * chunks : (block + 1) * chunks].astype(out_ref.dtype)
    slots, owned = assign_ref.shape
    spot = lax.broadcasted_iota(jnp.int32, (chunks, LANES), 1)
    codes = jnp.zeros((chunks, LANES), jnp.float32)
    for slot in range(slots):
        for within in range(owned):
            codes = jnp.where(spot == slot * owned + within, assign_ref[slot, within].astype(jnp.float32), codes)
    out_ref[blocks] = codes.astype(out_ref.dtype)
    groups = band_ref.shape[1] // offs
    tiles = meta_ref.shape[0] // offs
    spot = lax.broadcasted_iota(jnp.int32, (SUB, LANES), 1)
    here = (off_ref[0] * owned + (spot // groups)) * pitch
    flags = jnp.full((SUB, LANES), (offs * owned * pitch) << CODE_SHIFT, jnp.int32)
    for within in range(owned):
        flags = jnp.where(spot == owned * groups + within, aperture_ref[0, within], flags)
    for owner in range(offs):
        first = jnp.zeros((SUB, LANES), jnp.int32)
        for within in range(owned):
            for group in range(groups):
                first = jnp.where(spot == within * groups + group, band_ref[within, owner * groups + group], first)
        code = ((here + (first >> 7)) << CODE_SHIFT) | ((-first) & (LANES - 1))
        row = jnp.where(spot < owned * groups, code, flags)
        for tile in range(0, tiles, SUB):
            meta_ref[owner * tiles + tile : owner * tiles + tile + SUB] = row


def stack_kernel(at_ref, meta_ref, *refs, pieces, blocks, chunks, per_off, tiles, groups, window):
    piece_refs = refs[:pieces]
    out_ref, sums_ref, traces_ref, rows_ref, pairs_ref, words_ref, codes_ref, list_ref, sems, out_sems = refs[pieces:]
    slots = SUB
    parts = window // LANES
    halves = parts // 2
    pitch = chunks - halves + 1
    for piece in range(pieces):
        words_ref[piece : piece + 1] = piece_refs[piece][blocks, 0:1, :].astype(jnp.float32).astype(jnp.int32)
    fetch = pltpu.make_async_copy(words_ref, codes_ref, sems.at[pieces])
    fetch.start()
    copies = [
        pltpu.make_async_copy(piece_refs[piece], traces_ref.at[at_ref[piece]], sems.at[piece]) for piece in range(pieces)
    ]
    for copy in copies:
        copy.start()
    lane = lax.broadcasted_iota(jnp.int32, (2 * slots, LANES), 1).astype(MASK)
    zeros = jnp.zeros((2 * slots, LANES), jnp.bfloat16)
    for step in range(pitch):
        pairs_ref[blocks * pitch + step] = zeros
    for turn in range(2):
        rows_ref[turn, chunks * slots :] = jnp.zeros((slots, LANES), jnp.float32)
    for copy in copies:
        copy.wait()
    fetch.wait()

    def place(owner, carry):
        held = [at_ref[pieces + owner * 2 + half] for half in range(2)]
        for within in range(per_off):
            block = owner * per_off + within
            turn = within % 2
            for slot in range(slots):
                source = codes_ref[held[slot // 4], (slot % 4) * per_off + within] * 2 + slot // 4
                rows_ref[turn, pl.ds(slot, chunks, stride=slots), :] = traces_ref[source, block].astype(jnp.float32)
            start = block * pitch
            for step in range(pitch):
                near = rows_ref[turn, step * slots : (step + 1) * slots]
                far = rows_ref[turn, (step + halves) * slots : (step + halves + 1) * slots]
                pairs_ref[start + step] = jnp.concatenate([near, far], axis=0).astype(jnp.bfloat16)
        return carry

    lax.fori_loop(0, blocks // per_off, place, 0)

    def one_tile(tile, carry):
        count = 0
        for block in range(blocks):
            row = ((block // per_off) * tiles + tile) * LANES
            within = block % per_off
            list_ref[count] = row + within * groups
            count = count + meta_ref[row + per_off * groups + within]
        for more in range(TURNS - 1):
            list_ref[count + more] = per_off * groups + per_off

        def add(step, sums):
            sums = list(sums)
            for turn in range(TURNS):
                entry = list_ref[TURNS * step + turn]
                for group in range(groups):
                    code = meta_ref[entry + group]
                    base = code >> CODE_SHIFT
                    back = code & (LANES - 1)
                    mask = lane >= ((-jnp.broadcast_to(code, (2 * slots, LANES))) & (LANES - 1)).astype(MASK)
                    piece = [pairs_ref[base + step_] for step_ in range(halves + 1)]
                    for part in range(halves):
                        mixed = jnp.where(mask, piece[part], piece[part + 1])
                        turned = pltpu.roll(mixed, back, 1).astype(jnp.float32)
                        for side in range(2):
                            sums[group * parts + side * halves + part] += turned[side * slots : (side + 1) * slots]
            return tuple(sums)

        zero = tuple(jnp.zeros((slots, LANES), jnp.float32) for _ in range(groups * parts))
        sums = lax.fori_loop(0, (count + TURNS - 1) // TURNS, add, zero)
        for group in range(groups):
            for part in range(parts):
                sums_ref[tile, group, :, part * LANES : (part + 1) * LANES] = sums[group * parts + part].astype(jnp.bfloat16)
        pltpu.make_async_copy(sums_ref.at[tile], out_ref.at[tile], out_sems.at[tile]).start()
        return carry

    lax.fori_loop(0, tiles, one_tile, 0)
    for tile in range(tiles):
        pltpu.make_async_copy(sums_ref.at[tile], out_ref.at[tile], out_sems.at[tile]).wait()


def image_kernel(off_ref, stacked_ref, interp_ref, amp_ref, *refs, scale):
    *out_refs, image_ref = refs
    sources, groups, slots, window = stacked_ref.shape
    rows, pixels = out_refs[0].shape
    pixels = pixels // groups
    for group in range(groups):
        stacked = stacked_ref[:, group].reshape(sources * slots, window)
        depth = lax.dot_general(interp_ref[group], stacked, (((1,), (1,)), ((), ())), preferred_element_type=jnp.float32)
        high = depth.astype(jnp.bfloat16)
        low = (depth - high.astype(jnp.float32)).astype(jnp.bfloat16)
        amp = amp_ref[group]
        image = jnp.dot(high, amp, preferred_element_type=jnp.float32) + jnp.dot(low, amp, preferred_element_type=jnp.float32)
        image_ref[:, group * pixels : (group + 1) * pixels] = image * scale
    for apart, ref in enumerate(out_refs):
        ref[...] = image_ref[pl.ds(pl.multiple_of((off_ref[0] ^ apart) * rows, rows), rows), :].astype(ref.dtype)


def join_kernel(off_ref, *refs):
    out_ref = refs[-1]
    for apart, ref in enumerate(refs[:-1]):
        width = ref.shape[1]
        start = pl.multiple_of((off_ref[0] ^ apart) * width, LANES)
        out_ref[:, pl.ds(start, width)] = ref[...].astype(out_ref.dtype)


def ring_pairs(step):
    return [(z, (z + step) % 4) for z in range(4)]


def local(shot_traces, assign, aperture, band, interp, amp):
    blocks, samples = shot_traces.shape[1], shot_traces.shape[3]
    per_off, all_groups = band.shape
    offs = blocks // per_off
    groups = all_groups // offs
    tiles = lax.axis_size("x") * lax.axis_size("y")
    window, depth = interp.shape[1], interp.shape[2]
    pixels = amp.shape[2]
    chunks = samples // LANES
    zh, core, zl = lax.axis_index("zh"), lax.axis_index("core"), lax.axis_index("zl")
    z = zh * 2 + zl
    off = zh * 2 + core
    swap = [(0, 1), (1, 0)]

    smem = pl.BlockSpec(memory_space=pltpu.SMEM)
    vmem = pl.BlockSpec(memory_space=pltpu.VMEM)
    anywhere = pl.BlockSpec(memory_space=pl.ANY)

    pitch = chunks - window // LANES // 2 + 1
    sent, row = pl.pallas_call(
        functools.partial(prepare_kernel, offs=offs, pitch=pitch),
        out_shape=[
            pltpu.VMEM((blocks + 1, chunks, LANES), jnp.bfloat16),
            pltpu.VMEM((offs * tiles, LANES), jnp.int32),
        ],
        in_specs=[smem, smem, smem, smem, vmem],
        out_specs=[vmem, vmem],
        scratch_shapes=[pltpu.VMEM((blocks * chunks, LANES), jnp.float32)],
        name="prepare_traces",
    )(off.reshape(1), jnp.transpose(assign[:, 0, :]), band, jnp.transpose(aperture), shot_traces[0, :, 0, :])
    steps = (1, 3, 2)
    ring = [lax.ppermute(sent, ("zh", "zl"), ring_pairs(step)) for step in steps]

    meta = lax.all_to_all(row, OFF + PLANE, 0, 0, tiled=True)

    *ring, meta = lax.optimization_barrier((*ring, meta))
    column = [sent, *ring]
    pieces = column + [lax.ppermute(piece, "core", swap) for piece in column]
    at = [None] * len(pieces)
    where = [0] * len(pieces)
    for turn in range(2):
        for index, step in enumerate((0,) + steps):
            from_z = (z - step) % 4
            spot = (from_z // 2) * 4 + (core ^ turn) * 2 + from_z % 2
            at[turn * 4 + index] = spot
            for want in range(len(pieces)):
                where[want] = where[want] + jnp.where(spot == want, turn * 4 + index, 0)
    at = jnp.stack(at + where).astype(jnp.int32)

    stacked = pl.pallas_call(
        functools.partial(
            stack_kernel, pieces=len(pieces), blocks=blocks, chunks=chunks, per_off=per_off, tiles=tiles, groups=groups, window=window
        ),
        out_shape=jax.ShapeDtypeStruct((tiles, groups, SUB, window), jnp.bfloat16),
        in_specs=[smem, smem] + [vmem] * len(pieces),
        out_specs=anywhere,
        scratch_shapes=[
            pltpu.VMEM((tiles, groups, SUB, window), jnp.bfloat16),
            pltpu.VMEM((len(pieces), blocks + 1, chunks, LANES), jnp.bfloat16),
            pltpu.VMEM((2, (chunks + 1) * SUB, LANES), jnp.float32),
            pltpu.VMEM(((blocks + 1) * pitch, 2 * SUB, LANES), jnp.bfloat16),
            pltpu.VMEM((len(pieces), LANES), jnp.int32),
            pltpu.SMEM((len(pieces), LANES), jnp.int32),
            pltpu.SMEM((blocks + TURNS - 1,), jnp.int32),
            pltpu.SemaphoreType.DMA((len(pieces) + 1,)),
            pltpu.SemaphoreType.DMA((tiles,)),
        ],
        name="stack_windows",
    )(at, meta.reshape(-1), *map(in_vmem, pieces))

    arrived = lax.all_to_all(stacked, PLANE, 0, 0, tiled=True)

    interp_here = lax.dynamic_slice_in_dim(jnp.swapaxes(interp, 1, 2), off * groups, groups, 0)
    amp_here = lax.dynamic_slice_in_dim(amp, off * groups, groups, 0)
    strip = (depth // offs, groups * pixels)
    own, beside, far, across = pl.pallas_call(
        functools.partial(image_kernel, scale=1.0 / math.sqrt(blocks)),
        out_shape=[pltpu.VMEM(strip, jnp.float32)] + [pltpu.VMEM(strip, jnp.bfloat16)] * 3,
        in_specs=[smem, vmem, vmem, vmem],
        out_specs=[vmem] * 4,
        scratch_shapes=[pltpu.VMEM((depth, groups * pixels), jnp.float32)],
        name="image_groups",
    )(off.reshape(1), in_vmem(arrived), in_vmem(interp_here), in_vmem(amp_here))

    beside = lax.ppermute(beside, "core", swap)
    far = lax.ppermute(far, "zh", swap)
    across = lax.ppermute(across, OFF, [(index, index ^ 3) for index in range(offs)])
    return pl.pallas_call(
        join_kernel,
        out_shape=jax.ShapeDtypeStruct((depth // offs, offs * groups * pixels), jnp.float32),
        in_specs=[smem] + [vmem] * 4,
        out_specs=vmem,
        name="join_groups",
    )(off.reshape(1), *map(in_vmem, (own, beside, far, across)))


def solution(mesh):
    fine = Mesh(mesh.devices.reshape(2, 2, 4, 4, 2), EVERY)
    placed = (
        P(OFF, None, IMG, None),
        P(OFF, IMG, None),
        P(OFF, IMG),
        P(OFF, IMG),
        P(IMG, None, None),
        P(IMG, None, None),
    )
    return jax.shard_map(local, mesh=fine, in_specs=placed, out_specs=P(OFF, IMG), check_vma=False)
```

profile of v0, /device:TPU:1, one launch (start us, length us, event | category | flops | bytes accessed | tf_op | source)
XLA Modules:
  0.0 73.7 jit_solution(14688832314477835444)
XLA Ops:
  0.0 0.0 copy-start
  0.0 2.4 %prepare_traces.1 = (bf16[33,32,128]{2,1,0:T(8,128)(2,1)S(1)}, s32[64,128]{1,0:T(8,128)}) custom-call(s32[1]{0:T(128)} %bitcast.off_ref, s32[4,8]{1,0:T(4,128)} %bitcast.31, s32[8,32]{1,0:T(8,128)} %band_ref.1, s32[1,8]{1,0:T(1,128)} %bitcast.32, bf16[32,4096]{1,0:T(8,128)(2,1)} %bitcast.29), custom_call_target="tpu_custom_call" | custom-call | tf_op jit(solution)/shard_map/prepare_traces/pallas_call | solution.py:194
  2.4 2.5 %collective-permute-start = (bf16[33,32,128]{2,1,0:T(8,128)(2,1)S(1)}, bf16[33,32,128]{2,1,0:T(8,128)(2,1)S(1)}, u32[]{:S(2)}, u32[]{:S(2)}) collective-permute-start(bf16[33,32,128]{2,1,0:T(8,128)(2,1)S(1)} %get-tuple-element.15.refs_0_), channel_id=1, source_target_pairs={{0,1},{1,64},{64,65},{65,0},{2,3},{3,66},{66,67},{67,2},{4,5},{5,6... | collective-permute-start | bytes 811016 | tf_op jit(solution)/shard_map/ppermute | solution.py:206
  4.8 2.1 %collective-permute-start.1 = (bf16[33,32,128]{2,1,0:T(8,128)(2,1)S(1)}, bf16[33,32,128]{2,1,0:T(8,128)(2,1)S(1)}, u32[]{:S(2)}, u32[]{:S(2)}) collective-permute-start(bf16[33,32,128]{2,1,0:T(8,128)(2,1)S(1)} %get-tuple-element.15.refs_0_), channel_id=1, source_target_pairs={{0,65},{1,0},{64,1},{65,64},{2,67},{3,2},{66,3},{67,66},{4,69},{5,... | collective-permute-start | bytes 811016 | tf_op jit(solution)/shard_map/ppermute | solution.py:206
  7.0 1.3 %collective-permute-start.2 = (bf16[33,32,128]{2,1,0:T(8,128)(2,1)S(1)}, bf16[33,32,128]{2,1,0:T(8,128)(2,1)S(1)}, u32[]{:S(2)}, u32[]{:S(2)}) collective-permute-start(bf16[33,32,128]{2,1,0:T(8,128)(2,1)S(1)} %get-tuple-element.15.refs_0_), channel_id=1, source_target_pairs={{0,64},{1,65},{64,0},{65,1},{2,66},{3,67},{66,2},{67,3},{4,68},{5,... | collective-permute-start | bytes 811016 | tf_op jit(solution)/shard_map/ppermute | solution.py:206
  8.3 10.1 %all-to-all-start = ((s32[64,1,128]{2,1,0:T(1,128)}), s32[64,1,128]{2,1,0:T(1,128)S(1)}, u32[]{:S(2)}, u32[]{:S(2)}) async-start(s32[64,1,128]{2,1,0:T(1,128)} %bitcast.22), calls=%async_computation | async-start | bytes 65536 | tf_op jit(solution)/shard_map/all_to_all | solution.py:208
  18.4 0.5 collective-permute-start.3
  18.9 8.7 %all-to-all-done = s32[64,1,128]{2,1,0:T(1,128)S(1)} async-done(((s32[64,1,128]{2,1,0:T(1,128)}), s32[64,1,128]{2,1,0:T(1,128)S(1)}, u32[]{:S(2)}, u32[]{:S(2)}) %all-to-all-start) | async-done | bytes 32800 | tf_op jit(solution)/shard_map/all_to_all | solution.py:208
  27.6 0.0 copy-start.1
  27.6 0.0 collective-permute-done.refs_1_
  27.6 0.0 collective-permute-done.1.refs_2_
  27.6 0.0 collective-permute-done.2.refs_3_
  27.6 0.7 collective-permute-start.4
  28.3 0.1 collective-permute-start.5
  28.4 0.4 collective-permute-start.6
  28.8 0.6 stack.67.at_ref
  29.4 0.0 collective-permute-done.3.refs_4_
  29.4 0.0 collective-permute-done.4.refs_5_
  29.5 0.4 collective-permute-done.5.refs_6_
  29.9 0.4 collective-permute-done.6.refs_7_
  30.2 0.0 copy-done.1
  30.2 12.8 %stack_windows.1 = bf16[16,8,8,512]{3,2,1,0:T(8,128)(2,1)} custom-call(s32[16]{0:T(128)} %stack.67.at_ref, s32[8192]{0:T(1024)} %bitcast.30, bf16[33,32,128]{2,1,0:T(8,128)(2,1)S(1)} %get-tuple-element.15.refs_0_, bf16[33,32,128]{2,1,0:T(8,128)(2,1)S(1)} %collective-permute-done.refs_1_, bf16[33,32,128]{2,1,0:T(8,128)(2,1)S(1)} %collective-permute-done.1.refs_2_, ...), custom_call_target="tpu_custom_call" | custom-call | tf_op jit(solution)/shard_map/stack_windows/pallas_call | solution.py:224
  43.0 3.7 %all-to-all-start.1 = ((bf16[16,8,8,512]{3,2,1,0:T(8,128)(2,1)}), bf16[16,8,8,512]{3,2,1,0:T(8,128)(2,1)S(1)}, u32[]{:S(2)}, u32[]{:S(2)}) async-start(bf16[16,8,8,512]{3,2,1,0:T(8,128)(2,1)} %stack_windows.1), calls=%async_computation.1 | async-start | bytes 2097152 | tf_op jit(solution)/shard_map/all_to_all | solution.py:245
  46.7 0.0 copy-done
  46.8 1.1 %dynamic-slice_bitcast_fusion.interp_ref = bf16[8,64,512]{2,1,0:T(8,128)(2,1)S(1)} fusion(bf16[32,512,64]{1,2,0:T(8,128)(2,1)} %param.10, s32[]{:T(128)S(6)} %select_n.317), kind=kLoop, calls=%fused_computation | loop fusion | bytes 1048580 | tf_op jit(solution)/shard_map/dynamic_slice | solution.py:247
  47.9 15.4 %all-to-all-done.1.stacked_ref = bf16[16,8,8,512]{3,2,1,0:T(8,128)(2,1)S(1)} async-done(((bf16[16,8,8,512]{3,2,1,0:T(8,128)(2,1)}), bf16[16,8,8,512]{3,2,1,0:T(8,128)(2,1)S(1)}, u32[]{:S(2)}, u32[]{:S(2)}) %all-to-all-start.1) | async-done | bytes 1048608 | tf_op jit(solution)/shard_map/all_to_all | solution.py:245
  63.3 1.8 %image_groups.1 = (f32[16,1024]{1,0:T(8,128)S(1)}, bf16[16,1024]{1,0:T(8,128)(2,1)S(1)}, bf16[16,1024]{1,0:T(8,128)(2,1)S(1)}, bf16[16,1024]{1,0:T(8,128)(2,1)S(1)}) custom-call(s32[1]{0:T(128)} %bitcast.off_ref, bf16[16,8,8,512]{3,2,1,0:T(8,128)(2,1)S(1)} %all-to-all-done.1.stacked_ref, bf16[8,64,512]{2,1,0:T(8,128)(2,1)S(1)} %dynamic-slice_bitcast_fusion.interp_ref, ...), custom_call_target="tpu_custom_call" | custom-call | tf_op jit(solution)/shard_map/image_groups/pallas_call | solution.py:250
  65.1 2.2 %collective-permute-start.7 = (bf16[16,1024]{1,0:T(8,128)(2,1)S(1)}, bf16[16,1024]{1,0:T(8,128)(2,1)S(1)}, u32[]{:S(2)}, u32[]{:S(2)}) collective-permute-start(bf16[16,1024]{1,0:T(8,128)(2,1)S(1)} %get-tuple-element.22), channel_id=1, source_target_pairs={{0,32},{32,0},{1,33},{33,1},{2,34},{34,2},{3,35},{35,3},{4,36},{36... | collective-permute-start | bytes 98312 | tf_op jit(solution)/shard_map/ppermute | solution.py:259
  67.3 0.5 collective-permute-start.8
  67.8 2.7 %collective-permute-start.9 = (bf16[16,1024]{1,0:T(8,128)(2,1)S(1)}, bf16[16,1024]{1,0:T(8,128)(2,1)S(1)}, u32[]{:S(2)}, u32[]{:S(2)}) collective-permute-start(bf16[16,1024]{1,0:T(8,128)(2,1)S(1)} %get-tuple-element.24), channel_id=1, source_target_pairs={{0,96},{32,64},{64,32},{96,0},{1,97},{33,65},{65,33},{97,1},{2,98}... | collective-permute-start | bytes 98312 | tf_op jit(solution)/shard_map/ppermute | solution.py:261
  70.6 0.0 collective-permute-done.7.refs_1_
  70.6 1.1 %collective-permute-done.8.refs_2_ = bf16[16,1024]{1,0:T(8,128)(2,1)S(1)} collective-permute-done((bf16[16,1024]{1,0:T(8,128)(2,1)S(1)}, bf16[16,1024]{1,0:T(8,128)(2,1)S(1)}, u32[]{:S(2)}, u32[]{:S(2)}) %collective-permute-start.8) | collective-permute-done | bytes 32800 | tf_op jit(solution)/shard_map/ppermute | solution.py:260
  71.6 1.4 %collective-permute-done.9.refs_3_ = bf16[16,1024]{1,0:T(8,128)(2,1)S(1)} collective-permute-done((bf16[16,1024]{1,0:T(8,128)(2,1)S(1)}, bf16[16,1024]{1,0:T(8,128)(2,1)S(1)}, u32[]{:S(2)}, u32[]{:S(2)}) %collective-permute-start.9) | collective-permute-done | bytes 32800 | tf_op jit(solution)/shard_map/ppermute | solution.py:261
  73.0 0.7 join_groups.1
  (1 shorter events, 0.0 us)
Async XLA Ops:
  0.0 46.7 %copy-start = (bf16[32,128,128]{2,1,0:T(8,128)(2,1)S(1)}, bf16[32,128,128]{2,1,0:T(8,128)(2,1)}, u32[]{:S(2)}) copy-start(bf16[32,128,128]{2,1,0:T(8,128)(2,1)} %param.11) | copy-start | bytes 3145732
  2.4 25.2 %collective-permute-start = (bf16[33,32,128]{2,1,0:T(8,128)(2,1)S(1)}, bf16[33,32,128]{2,1,0:T(8,128)(2,1)S(1)}, u32[]{:S(2)}, u32[]{:S(2)}) collective-permute-start(bf16[33,32,128]{2,1,0:T(8,128)(2,1)S(1)} %get-tuple-element.15.refs_0_), channel_id=1, source_target_pairs={{0,1},{1,64},{64,65},{65,0},{2,3},{3,66},{66,67},{67,2},{4,5},{5,6... | collective-permute-start | bytes 811016 | tf_op jit(solution)/shard_map/ppermute | solution.py:206
  4.8 22.7 %collective-permute-start.1 = (bf16[33,32,128]{2,1,0:T(8,128)(2,1)S(1)}, bf16[33,32,128]{2,1,0:T(8,128)(2,1)S(1)}, u32[]{:S(2)}, u32[]{:S(2)}) collective-permute-start(bf16[33,32,128]{2,1,0:T(8,128)(2,1)S(1)} %get-tuple-element.15.refs_0_), channel_id=1, source_target_pairs={{0,65},{1,0},{64,1},{65,64},{2,67},{3,2},{66,3},{67,66},{4,69},{5,... | collective-permute-start | bytes 811016 | tf_op jit(solution)/shard_map/ppermute | solution.py:206
  7.0 20.6 %collective-permute-start.2 = (bf16[33,32,128]{2,1,0:T(8,128)(2,1)S(1)}, bf16[33,32,128]{2,1,0:T(8,128)(2,1)S(1)}, u32[]{:S(2)}, u32[]{:S(2)}) collective-permute-start(bf16[33,32,128]{2,1,0:T(8,128)(2,1)S(1)} %get-tuple-element.15.refs_0_), channel_id=1, source_target_pairs={{0,64},{1,65},{64,0},{65,1},{2,66},{3,67},{66,2},{67,3},{4,68},{5,... | collective-permute-start | bytes 811016 | tf_op jit(solution)/shard_map/ppermute | solution.py:206
  8.3 19.3 %all-to-all-start = ((s32[64,1,128]{2,1,0:T(1,128)}), s32[64,1,128]{2,1,0:T(1,128)S(1)}, u32[]{:S(2)}, u32[]{:S(2)}) async-start(s32[64,1,128]{2,1,0:T(1,128)} %bitcast.22), calls=%async_computation | async-start | bytes 65536 | tf_op jit(solution)/shard_map/all_to_all | solution.py:208
  18.4 11.1 %collective-permute-start.3 = (bf16[33,32,128]{2,1,0:T(8,128)(2,1)S(1)}, bf16[33,32,128]{2,1,0:T(8,128)(2,1)S(1)}, u32[]{:S(2)}, u32[]{:S(2)}) collective-permute-start(bf16[33,32,128]{2,1,0:T(8,128)(2,1)S(1)} %get-tuple-element.15.refs_0_), channel_id=1, source_target_pairs={{0,32},{32,0},{1,33},{33,1},{2,34},{34,2},{3,35},{35,3},{4,36},{36... | collective-permute-start | bytes 811016 | tf_op jit(solution)/shard_map/ppermute | solution.py:212
  27.6 2.7 %copy-start.1 = (s32[64,1,128]{2,1,0:T(1,128)}, s32[64,1,128]{2,1,0:T(1,128)S(1)}, u32[]{:S(2)}) copy-start(s32[64,1,128]{2,1,0:T(1,128)S(1)} %all-to-all-done) | copy-start | bytes 98308
  27.6 1.9 %collective-permute-start.4 = (bf16[33,32,128]{2,1,0:T(8,128)(2,1)S(1)}, bf16[33,32,128]{2,1,0:T(8,128)(2,1)S(1)}, u32[]{:S(2)}, u32[]{:S(2)}) collective-permute-start(bf16[33,32,128]{2,1,0:T(8,128)(2,1)S(1)} %collective-permute-done.refs_1_), channel_id=1, source_target_pairs={{0,32},{32,0},{1,33},{33,1},{2,34},{34,2},{3,35},{35,3},{4,36},{36... | collective-permute-start | bytes 811016 | tf_op jit(solution)/shard_map/ppermute | solution.py:212
  28.3 1.6 %collective-permute-start.5 = (bf16[33,32,128]{2,1,0:T(8,128)(2,1)S(1)}, bf16[33,32,128]{2,1,0:T(8,128)(2,1)S(1)}, u32[]{:S(2)}, u32[]{:S(2)}) collective-permute-start(bf16[33,32,128]{2,1,0:T(8,128)(2,1)S(1)} %collective-permute-done.1.refs_2_), channel_id=1, source_target_pairs={{0,32},{32,0},{1,33},{33,1},{2,34},{34,2},{3,35},{35,3},{4,36},{36... | collective-permute-start | bytes 811016 | tf_op jit(solution)/shard_map/ppermute | solution.py:212
  28.4 1.9 %collective-permute-start.6 = (bf16[33,32,128]{2,1,0:T(8,128)(2,1)S(1)}, bf16[33,32,128]{2,1,0:T(8,128)(2,1)S(1)}, u32[]{:S(2)}, u32[]{:S(2)}) collective-permute-start(bf16[33,32,128]{2,1,0:T(8,128)(2,1)S(1)} %collective-permute-done.2.refs_3_), channel_id=1, source_target_pairs={{0,32},{32,0},{1,33},{33,1},{2,34},{34,2},{3,35},{35,3},{4,36},{36... | collective-permute-start | bytes 811016 | tf_op jit(solution)/shard_map/ppermute | solution.py:212
  43.0 20.2 %all-to-all-start.1 = ((bf16[16,8,8,512]{3,2,1,0:T(8,128)(2,1)}), bf16[16,8,8,512]{3,2,1,0:T(8,128)(2,1)S(1)}, u32[]{:S(2)}, u32[]{:S(2)}) async-start(bf16[16,8,8,512]{3,2,1,0:T(8,128)(2,1)} %stack_windows.1), calls=%async_computation.1 | async-start | bytes 2097152 | tf_op jit(solution)/shard_map/all_to_all | solution.py:245
  65.1 5.5 %collective-permute-start.7 = (bf16[16,1024]{1,0:T(8,128)(2,1)S(1)}, bf16[16,1024]{1,0:T(8,128)(2,1)S(1)}, u32[]{:S(2)}, u32[]{:S(2)}) collective-permute-start(bf16[16,1024]{1,0:T(8,128)(2,1)S(1)} %get-tuple-element.22), channel_id=1, source_target_pairs={{0,32},{32,0},{1,33},{33,1},{2,34},{34,2},{3,35},{35,3},{4,36},{36... | collective-permute-start | bytes 98312 | tf_op jit(solution)/shard_map/ppermute | solution.py:259
  67.3 4.3 %collective-permute-start.8 = (bf16[16,1024]{1,0:T(8,128)(2,1)S(1)}, bf16[16,1024]{1,0:T(8,128)(2,1)S(1)}, u32[]{:S(2)}, u32[]{:S(2)}) collective-permute-start(bf16[16,1024]{1,0:T(8,128)(2,1)S(1)} %get-tuple-element.23), channel_id=1, source_target_pairs={{0,64},{64,0},{1,65},{65,1},{2,66},{66,2},{3,67},{67,3},{4,68},{68... | collective-permute-start | bytes 98312 | tf_op jit(solution)/shard_map/ppermute | solution.py:260
  67.8 5.2 %collective-permute-start.9 = (bf16[16,1024]{1,0:T(8,128)(2,1)S(1)}, bf16[16,1024]{1,0:T(8,128)(2,1)S(1)}, u32[]{:S(2)}, u32[]{:S(2)}) collective-permute-start(bf16[16,1024]{1,0:T(8,128)(2,1)S(1)} %get-tuple-element.24), channel_id=1, source_target_pairs={{0,96},{32,64},{64,32},{96,0},{1,97},{33,65},{65,33},{97,1},{2,98}... | collective-permute-start | bytes 98312 | tf_op jit(solution)/shard_map/ppermute | solution.py:261
where the time goes:
time: 74.7 us; the launch traced here: 73.7 us
  waiting for transfers between devices  27.3 us (37%)
  starting transfers between devices  26.9 us (36%)
  Pallas kernels  17.7 us (24%)
  local copies, waits for them, and re-layouts  1.74 us (2%)
    all_to_all x1, waiting for transfers between devices, local(): arrived = lax.all_to_all(stacked, PLANE, 0, 0, tiled=True)  15.4 us
    pallas_call x1, Pallas kernels, local(): pl.pallas_call(functools.partial(stack_kernel, pieces=len(pieces), blocks...  12.8 us
    all_to_all x1, starting transfers between devices, local(): meta = lax.all_to_all(row, OFF + PLANE, 0, 0, tiled=True)  10.1 us
    all_to_all x1, waiting for transfers between devices, local(): meta = lax.all_to_all(row, OFF + PLANE, 0, 0, tiled=True)  8.66 us
    ppermute x3, starting transfers between devices, local(): lax.ppermute(sent, ('zh', 'zl'), ring_pairs(step))  5.89 us
    all_to_all x1, starting transfers between devices, local(): arrived = lax.all_to_all(stacked, PLANE, 0, 0, tiled=True)  3.66 us
    ppermute x1, starting transfers between devices, local(): lax.ppermute(across, OFF, [(index, index ^ 3) for index in range(offs)])  2.74 us
    pallas_call x1, Pallas kernels, local(): pl.pallas_call(functools.partial(prepare_kernel, offs=offs, pitch=pitch),...  2.36 us
  transfers between devices with their start and end apart: 12, of which 6 were waited for; matrix products, arithmetic and copies ran while one was open for 2% of the time, Pallas kernels for 0%

commit v1 on v0

--- a/solution.py
+++ b/solution.py
@@ -15,7 +15,7 @@
 IMG = ("x", "y", "zl")
 EVERY = OFF + IMG
 CODE_SHIFT = 7
-TURNS = 8
+TURNS = (16, 8)
 MASK = jnp.int16
 
 
@@ -23,7 +23,37 @@
     return pltpu.with_memory_space_constraint(array, pltpu.VMEM)
 
 
-def prepare_kernel(off_ref, assign_ref, band_ref, aperture_ref, traces_ref, out_ref, meta_ref, rows_ref, *, offs, pitch):
+def code_rows(off_ref, band_ref, aperture_ref, meta_ref, *, offs, owned, pitch):
+    groups = band_ref.shape[1] // offs
+    spot = lax.broadcasted_iota(jnp.int32, (SUB, LANES), 1)
+    line = lax.broadcasted_iota(jnp.int32, (SUB, LANES), 0)
+    here = (off_ref[0] * owned + (spot // groups)) * pitch
+    flags = jnp.full((SUB, LANES), (offs * owned * pitch) << CODE_SHIFT, jnp.int32)
+    for within in range(owned):
+        flags = jnp.where(spot == owned * groups + within, aperture_ref[0, within], flags)
+    first = jnp.zeros((SUB, LANES), jnp.int32)
+    for within in range(owned):
+        for group in range(groups):
+            values = jnp.zeros((SUB, LANES), jnp.int32)
+            for owner in range(offs):
+                values = jnp.where(line == owner, band_ref[within, owner * groups + group], values)
+            first = jnp.where(spot == within * groups + group, values, first)
+    code = ((here + (first >> 7)) << CODE_SHIFT) | ((-first) & (LANES - 1))
+    block = jnp.where(spot < owned * groups, code, flags)
+    tiles = meta_ref.shape[0] // offs
+    for owner in range(offs):
+        row = jnp.broadcast_to(block[owner : owner + 1], (SUB, LANES))
+        for tile in range(0, tiles, SUB):
+            meta_ref[owner * tiles + tile : owner * tiles + tile + SUB] = row
+
+
+def prepare_kernel(off_ref, assign_ref, band_ref, aperture_ref, raw_ref, out_ref, sent_ref, rows_ref, traces_ref, meta_ref, sems, *, offs, pitch):
+    fetch = pltpu.make_async_copy(raw_ref, traces_ref, sems.at[0])
+    fetch.start()
+    code_rows(off_ref, band_ref, aperture_ref, meta_ref, offs=offs, owned=assign_ref.shape[1], pitch=pitch)
+    send = pltpu.make_async_copy(meta_ref, sent_ref, sems.at[1])
+    send.start()
+    fetch.wait()
     blocks, samples = traces_ref.shape
     chunks = samples // LANES
     lane = lax.broadcasted_iota(jnp.int32, (blocks, LANES), 1)
@@ -42,37 +72,31 @@
         for within in range(owned):
             codes = jnp.where(spot == slot * owned + within, assign_ref[slot, within].astype(jnp.float32), codes)
     out_ref[blocks] = codes.astype(out_ref.dtype)
-    groups = band_ref.shape[1] // offs
-    tiles = meta_ref.shape[0] // offs
-    spot = lax.broadcasted_iota(jnp.int32, (SUB, LANES), 1)
-    here = (off_ref[0] * owned + (spot // groups)) * pitch
-    flags = jnp.full((SUB, LANES), (offs * owned * pitch) << CODE_SHIFT, jnp.int32)
-    for within in range(owned):
-        flags = jnp.where(spot == owned * groups + within, aperture_ref[0, within], flags)
-    for owner in range(offs):
-        first = jnp.zeros((SUB, LANES), jnp.int32)
-        for within in range(owned):
-            for group in range(groups):
-                first = jnp.where(spot == within * groups + group, band_ref[within, owner * groups + group], first)
-        code = ((here + (first >> 7)) << CODE_SHIFT) | ((-first) & (LANES - 1))
-        row = jnp.where(spot < owned * groups, code, flags)
-        for tile in range(0, tiles, SUB):
-            meta_ref[owner * tiles + tile : owner * tiles + tile + SUB] = row
-
-
-def stack_kernel(at_ref, meta_ref, *refs, pieces, blocks, chunks, per_off, tiles, groups, window):
+    send.wait()
+
+
+def spot_of(piece, z, core):
+    from_z = (z - ((piece % 4) ^ (piece % 4 >> 1))) & 3
+    return (from_z >> 1) * 4 + (core ^ (piece // 4)) * 2 + (from_z & 1)
+
+
+def stack_kernel(z_ref, core_ref, table_ref, *refs, pieces, blocks, chunks, per_off, tiles, groups, window):
     piece_refs = refs[:pieces]
-    out_ref, sums_ref, traces_ref, rows_ref, pairs_ref, words_ref, codes_ref, list_ref, sems, out_sems = refs[pieces:]
+    out_ref, sums_ref, traces_ref, rows_ref, pairs_ref, words_ref, codes_ref, meta_ref, list_ref, sems, out_sems = refs[pieces:]
+    table = pltpu.make_async_copy(table_ref, meta_ref, sems.at[pieces + 1])
+    table.start()
     slots = SUB
     parts = window // LANES
     halves = parts // 2
     pitch = chunks - halves + 1
+    z, core = z_ref[0], core_ref[0]
     for piece in range(pieces):
         words_ref[piece : piece + 1] = piece_refs[piece][blocks, 0:1, :].astype(jnp.float32).astype(jnp.int32)
     fetch = pltpu.make_async_copy(words_ref, codes_ref, sems.at[pieces])
     fetch.start()
     copies = [
-        pltpu.make_async_copy(piece_refs[piece], traces_ref.at[at_ref[piece]], sems.at[piece]) for piece in range(pieces)
+        pltpu.make_async_copy(piece_refs[piece], traces_ref.at[spot_of(piece, z, core)], sems.at[piece])
+        for piece in range(pieces)
     ]
     for copy in copies:
         copy.start()
@@ -87,7 +111,8 @@
     fetch.wait()
 
     def place(owner, carry):
-        held = [at_ref[pieces + owner * 2 + half] for half in range(2)]
+        steps = [(z - (owner >> 1) * 2 - half) & 3 for half in range(2)]
+        held = [(core ^ (owner & 1)) * 4 + (step ^ (step >> 1)) for step in steps]
         for within in range(per_off):
             block = owner * per_off + within
             turn = within % 2
@@ -102,6 +127,7 @@
         return carry
 
     lax.fori_loop(0, blocks // per_off, place, 0)
+    table.wait()
 
     def one_tile(tile, carry):
         count = 0
@@ -110,13 +136,13 @@
             within = block % per_off
             list_ref[count] = row + within * groups
             count = count + meta_ref[row + per_off * groups + within]
-        for more in range(TURNS - 1):
+        for more in range(TURNS[-1] - 1):
             list_ref[count + more] = per_off * groups + per_off
 
-        def add(step, sums):
+        def add(step, sums, done, turns):
             sums = list(sums)
-            for turn in range(TURNS):
-                entry = list_ref[TURNS * step + turn]
+            for turn in range(turns):
+                entry = list_ref[done + turns * step + turn]
                 for group in range(groups):
                     code = meta_ref[entry + group]
                     base = code >> CODE_SHIFT
@@ -131,7 +157,13 @@
             return tuple(sums)
 
         zero = tuple(jnp.zeros((slots, LANES), jnp.float32) for _ in range(groups * parts))
-        sums = lax.fori_loop(0, (count + TURNS - 1) // TURNS, add, zero)
+        sums, done = zero, 0
+        for turns in TURNS[:-1]:
+            steps = (count - done) // turns
+            sums = lax.fori_loop(0, steps, functools.partial(add, done=done, turns=turns), sums)
+            done = done + steps * turns
+        turns = TURNS[-1]
+        sums = lax.fori_loop(0, (count - done + turns - 1) // turns, functools.partial(add, done=done, turns=turns), sums)
         for group in range(groups):
             for part in range(parts):
                 sums_ref[tile, group, :, part * LANES : (part + 1) * LANES] = sums[group * parts + part].astype(jnp.bfloat16)
@@ -195,11 +227,16 @@
         functools.partial(prepare_kernel, offs=offs, pitch=pitch),
         out_shape=[
             pltpu.VMEM((blocks + 1, chunks, LANES), jnp.bfloat16),
+            jax.ShapeDtypeStruct((offs * tiles, LANES), jnp.int32),
+        ],
+        in_specs=[smem, smem, smem, smem, anywhere],
+        out_specs=[vmem, anywhere],
+        scratch_shapes=[
+            pltpu.VMEM((blocks * chunks, LANES), jnp.float32),
+            pltpu.VMEM((blocks, samples), jnp.bfloat16),
             pltpu.VMEM((offs * tiles, LANES), jnp.int32),
+            pltpu.SemaphoreType.DMA((2,)),
         ],
-        in_specs=[smem, smem, smem, smem, vmem],
-        out_specs=[vmem, vmem],
-        scratch_shapes=[pltpu.VMEM((blocks * chunks, LANES), jnp.float32)],
         name="prepare_traces",
     )(off.reshape(1), jnp.transpose(assign[:, 0, :]), band, jnp.transpose(aperture), shot_traces[0, :, 0, :])
     steps = (1, 3, 2)
@@ -210,23 +247,12 @@
     *ring, meta = lax.optimization_barrier((*ring, meta))
     column = [sent, *ring]
     pieces = column + [lax.ppermute(piece, "core", swap) for piece in column]
-    at = [None] * len(pieces)
-    where = [0] * len(pieces)
-    for turn in range(2):
-        for index, step in enumerate((0,) + steps):
-            from_z = (z - step) % 4
-            spot = (from_z // 2) * 4 + (core ^ turn) * 2 + from_z % 2
-            at[turn * 4 + index] = spot
-            for want in range(len(pieces)):
-                where[want] = where[want] + jnp.where(spot == want, turn * 4 + index, 0)
-    at = jnp.stack(at + where).astype(jnp.int32)
-
     stacked = pl.pallas_call(
         functools.partial(
             stack_kernel, pieces=len(pieces), blocks=blocks, chunks=chunks, per_off=per_off, tiles=tiles, groups=groups, window=window
         ),
         out_shape=jax.ShapeDtypeStruct((tiles, groups, SUB, window), jnp.bfloat16),
-        in_specs=[smem, smem] + [vmem] * len(pieces),
+        in_specs=[smem, smem, anywhere] + [vmem] * len(pieces),
         out_specs=anywhere,
         scratch_shapes=[
             pltpu.VMEM((tiles, groups, SUB, window), jnp.bfloat16),
@@ -235,12 +261,13 @@
             pltpu.VMEM(((blocks + 1) * pitch, 2 * SUB, LANES), jnp.bfloat16),
             pltpu.VMEM((len(pieces), LANES), jnp.int32),
             pltpu.SMEM((len(pieces), LANES), jnp.int32),
-            pltpu.SMEM((blocks + TURNS - 1,), jnp.int32),
-            pltpu.SemaphoreType.DMA((len(pieces) + 1,)),
+            pltpu.SMEM((offs * tiles * LANES,), jnp.int32),
+            pltpu.SMEM((blocks + TURNS[-1] - 1,), jnp.int32),
+            pltpu.SemaphoreType.DMA((len(pieces) + 2,)),
             pltpu.SemaphoreType.DMA((tiles,)),
         ],
         name="stack_windows",
-    )(at, meta.reshape(-1), *map(in_vmem, pieces))
+    )(z.reshape(1), core.reshape(1), in_vmem(meta.reshape(-1)), *map(in_vmem, pieces))
 
     arrived = lax.all_to_all(stacked, PLANE, 0, 0, tiled=True)
 

time: 74.7 us -> 74.2 us (level); the launches traced: 73.7 us -> 74.6 us
  transfers between devices with their start and end apart: 12 -> 12, of which waited for: 6 -> 7; matrix products, arithmetic and copies ran while one was open for 2% -> 1% of each run, Pallas kernels for 0% -> 0%
where the time goes in v1:
time: 74.2 us; the launch traced here: 74.6 us
  waiting for transfers between devices  27.9 us (38%)
  starting transfers between devices  27.1 us (37%)
  Pallas kernels  18.4 us (25%)
  local copies, waits for them, and re-layouts  1.12 us (2%)
    all_to_all x1, waiting for transfers between devices, local(): arrived = lax.all_to_all(stacked, PLANE, 0, 0, tiled=True)  15.4 us
    pallas_call x1, Pallas kernels, local(): pl.pallas_call(functools.partial(stack_kernel, pieces=len(pieces), blocks...  13.4 us
    all_to_all x1, starting transfers between devices, local(): meta = lax.all_to_all(row, OFF + PLANE, 0, 0, tiled=True)  10.2 us
    all_to_all x1, waiting for transfers between devices, local(): meta = lax.all_to_all(row, OFF + PLANE, 0, 0, tiled=True)  8.66 us
    ppermute x3, starting transfers between devices, local(): lax.ppermute(sent, ('zh', 'zl'), ring_pairs(step))  5.96 us
    all_to_all x1, starting transfers between devices, local(): arrived = lax.all_to_all(stacked, PLANE, 0, 0, tiled=True)  3.66 us
    ppermute x1, starting transfers between devices, local(): lax.ppermute(across, OFF, [(index, index ^ 3) for index in range(offs)])  2.72 us
    pallas_call x1, Pallas kernels, local(): pl.pallas_call(functools.partial(prepare_kernel, offs=offs, pitch=pitch),...  2.48 us
  transfers between devices with their start and end apart: 12, of which 7 were waited for; matrix products, arithmetic and copies ran while one was open for 1% of the time, Pallas kernels for 0%

profile of v1, /device:TPU:1, one launch (start us, length us, event | category | flops | bytes accessed | tf_op | source)
XLA Modules:
  0.0 74.6 jit_solution(6898648030962928256)
XLA Ops:
  0.0 0.0 copy-start
  0.0 2.5 %prepare_traces.1 = (bf16[33,32,128]{2,1,0:T(8,128)(2,1)S(1)}, s32[64,128]{1,0:T(8,128)}) custom-call(s32[1]{0:T(128)} %bitcast.off_ref, s32[4,8]{1,0:T(4,128)} %bitcast.18, s32[8,32]{1,0:T(8,128)} %band_ref.1, s32[1,8]{1,0:T(1,128)} %bitcast.19, bf16[32,4096]{1,0:T(8,128)(2,1)} %bitcast.16), custom_call_target="tpu_custom_call" | custom-call | tf_op jit(solution)/shard_map/prepare_traces/pallas_call | solution.py:226
  2.5 2.5 %collective-permute-start = (bf16[33,32,128]{2,1,0:T(8,128)(2,1)S(1)}, bf16[33,32,128]{2,1,0:T(8,128)(2,1)S(1)}, u32[]{:S(2)}, u32[]{:S(2)}) collective-permute-start(bf16[33,32,128]{2,1,0:T(8,128)(2,1)S(1)} %get-tuple-element.15.refs_0_), channel_id=1, source_target_pairs={{0,1},{1,64},{64,65},{65,0},{2,3},{3,66},{66,67},{67,2},{4,5},{5,6... | collective-permute-start | bytes 811016 | tf_op jit(solution)/shard_map/ppermute | solution.py:243
  5.0 2.2 %collective-permute-start.1 = (bf16[33,32,128]{2,1,0:T(8,128)(2,1)S(1)}, bf16[33,32,128]{2,1,0:T(8,128)(2,1)S(1)}, u32[]{:S(2)}, u32[]{:S(2)}) collective-permute-start(bf16[33,32,128]{2,1,0:T(8,128)(2,1)S(1)} %get-tuple-element.15.refs_0_), channel_id=1, source_target_pairs={{0,65},{1,0},{64,1},{65,64},{2,67},{3,2},{66,3},{67,66},{4,69},{5,... | collective-permute-start | bytes 811016 | tf_op jit(solution)/shard_map/ppermute | solution.py:243
  7.2 1.2 %collective-permute-start.2 = (bf16[33,32,128]{2,1,0:T(8,128)(2,1)S(1)}, bf16[33,32,128]{2,1,0:T(8,128)(2,1)S(1)}, u32[]{:S(2)}, u32[]{:S(2)}) collective-permute-start(bf16[33,32,128]{2,1,0:T(8,128)(2,1)S(1)} %get-tuple-element.15.refs_0_), channel_id=1, source_target_pairs={{0,64},{1,65},{64,0},{65,1},{2,66},{3,67},{66,2},{67,3},{4,68},{5,... | collective-permute-start | bytes 811016 | tf_op jit(solution)/shard_map/ppermute | solution.py:243
  8.5 10.2 %all-to-all-start = ((s32[64,1,128]{2,1,0:T(1,128)}), s32[64,1,128]{2,1,0:T(1,128)S(1)}, u32[]{:S(2)}, u32[]{:S(2)}) async-start(s32[64,1,128]{2,1,0:T(1,128)} %bitcast.17), calls=%async_computation | async-start | bytes 65536 | tf_op jit(solution)/shard_map/all_to_all | solution.py:245
  18.6 0.5 collective-permute-start.3
  19.2 8.7 %all-to-all-done = s32[64,1,128]{2,1,0:T(1,128)S(1)} async-done(((s32[64,1,128]{2,1,0:T(1,128)}), s32[64,1,128]{2,1,0:T(1,128)S(1)}, u32[]{:S(2)}, u32[]{:S(2)}) %all-to-all-start) | async-done | bytes 32800 | tf_op jit(solution)/shard_map/all_to_all | solution.py:245
  27.8 0.0 collective-permute-done.refs_1_
  27.8 0.0 collective-permute-done.1.refs_2_
  27.8 0.0 collective-permute-done.2.refs_3_
  27.9 0.7 collective-permute-start.4
  28.6 0.1 collective-permute-start.5
  28.7 0.4 collective-permute-start.6
  29.1 0.0 collective-permute-done.3.refs_4_
  29.1 0.7 collective-permute-done.4.refs_5_
  29.7 0.4 collective-permute-done.5.refs_6_
  30.1 0.4 collective-permute-done.6.refs_7_
  30.5 13.4 %stack_windows.1 = bf16[16,8,8,512]{3,2,1,0:T(8,128)(2,1)} custom-call(s32[1]{0:T(128)} %bitcast.1.z_ref, s32[1]{0:T(128)} %bitcast.2.core_ref, s32[8192]{0:T(1024)S(1)} %bitcast.15, bf16[33,32,128]{2,1,0:T(8,128)(2,1)S(1)} %get-tuple-element.15.refs_0_, bf16[33,32,128]{2,1,0:T(8,128)(2,1)S(1)} %collective-permute-done.refs_1_, ...), custom_call_target="tpu_custom_call" | custom-call | tf_op jit(solution)/shard_map/stack_windows/pallas_call | solution.py:250
  43.9 3.7 %all-to-all-start.1 = ((bf16[16,8,8,512]{3,2,1,0:T(8,128)(2,1)}), bf16[16,8,8,512]{3,2,1,0:T(8,128)(2,1)S(1)}, u32[]{:S(2)}, u32[]{:S(2)}) async-start(bf16[16,8,8,512]{3,2,1,0:T(8,128)(2,1)} %stack_windows.1), calls=%async_computation.1 | async-start | bytes 2097152 | tf_op jit(solution)/shard_map/all_to_all | solution.py:272
  47.6 0.0 copy-done
  47.6 1.1 %dynamic-slice_bitcast_fusion.interp_ref = bf16[8,64,512]{2,1,0:T(8,128)(2,1)S(1)} fusion(bf16[32,512,64]{1,2,0:T(8,128)(2,1)} %param.10, s32[]{:T(128)S(6)} %select_n.4), kind=kLoop, calls=%fused_computation | loop fusion | bytes 1048580 | tf_op jit(solution)/shard_map/dynamic_slice | solution.py:274
  48.7 15.4 %all-to-all-done.1.stacked_ref = bf16[16,8,8,512]{3,2,1,0:T(8,128)(2,1)S(1)} async-done(((bf16[16,8,8,512]{3,2,1,0:T(8,128)(2,1)}), bf16[16,8,8,512]{3,2,1,0:T(8,128)(2,1)S(1)}, u32[]{:S(2)}, u32[]{:S(2)}) %all-to-all-start.1) | async-done | bytes 1048608 | tf_op jit(solution)/shard_map/all_to_all | solution.py:272
  64.1 1.8 %image_groups.1 = (f32[16,1024]{1,0:T(8,128)S(1)}, bf16[16,1024]{1,0:T(8,128)(2,1)S(1)}, bf16[16,1024]{1,0:T(8,128)(2,1)S(1)}, bf16[16,1024]{1,0:T(8,128)(2,1)S(1)}) custom-call(s32[1]{0:T(128)} %bitcast.off_ref, bf16[16,8,8,512]{3,2,1,0:T(8,128)(2,1)S(1)} %all-to-all-done.1.stacked_ref, bf16[8,64,512]{2,1,0:T(8,128)(2,1)S(1)} %dynamic-slice_bitcast_fusion.interp_ref, ...), custom_call_target="tpu_custom_call" | custom-call | tf_op jit(solution)/shard_map/image_groups/pallas_call | solution.py:277
  65.9 2.3 %collective-permute-start.7 = (bf16[16,1024]{1,0:T(8,128)(2,1)S(1)}, bf16[16,1024]{1,0:T(8,128)(2,1)S(1)}, u32[]{:S(2)}, u32[]{:S(2)}) collective-permute-start(bf16[16,1024]{1,0:T(8,128)(2,1)S(1)} %get-tuple-element.22), channel_id=1, source_target_pairs={{0,32},{32,0},{1,33},{33,1},{2,34},{34,2},{3,35},{35,3},{4,36},{36... | collective-permute-start | bytes 98312 | tf_op jit(solution)/shard_map/ppermute | solution.py:286
  68.2 0.5 collective-permute-start.8
  68.7 2.7 %collective-permute-start.9 = (bf16[16,1024]{1,0:T(8,128)(2,1)S(1)}, bf16[16,1024]{1,0:T(8,128)(2,1)S(1)}, u32[]{:S(2)}, u32[]{:S(2)}) collective-permute-start(bf16[16,1024]{1,0:T(8,128)(2,1)S(1)} %get-tuple-element.24), channel_id=1, source_target_pairs={{0,96},{32,64},{64,32},{96,0},{1,97},{33,65},{65,33},{97,1},{2,98}... | collective-permute-start | bytes 98312 | tf_op jit(solution)/shard_map/ppermute | solution.py:288
  71.4 0.0 collective-permute-done.7.refs_1_
  71.4 1.1 %collective-permute-done.8.refs_2_ = bf16[16,1024]{1,0:T(8,128)(2,1)S(1)} collective-permute-done((bf16[16,1024]{1,0:T(8,128)(2,1)S(1)}, bf16[16,1024]{1,0:T(8,128)(2,1)S(1)}, u32[]{:S(2)}, u32[]{:S(2)}) %collective-permute-start.8) | collective-permute-done | bytes 32800 | tf_op jit(solution)/shard_map/ppermute | solution.py:287
  72.5 1.4 %collective-permute-done.9.refs_3_ = bf16[16,1024]{1,0:T(8,128)(2,1)S(1)} collective-permute-done((bf16[16,1024]{1,0:T(8,128)(2,1)S(1)}, bf16[16,1024]{1,0:T(8,128)(2,1)S(1)}, u32[]{:S(2)}, u32[]{:S(2)}) %collective-permute-start.9) | collective-permute-done | bytes 32800 | tf_op jit(solution)/shard_map/ppermute | solution.py:288
  73.8 0.7 join_groups.1
  (1 shorter events, 0.0 us)
Async XLA Ops:
  0.0 47.6 %copy-start = (bf16[32,128,128]{2,1,0:T(8,128)(2,1)S(1)}, bf16[32,128,128]{2,1,0:T(8,128)(2,1)}, u32[]{:S(2)}) copy-start(bf16[32,128,128]{2,1,0:T(8,128)(2,1)} %param.11) | copy-start | bytes 3145732
  2.5 25.4 %collective-permute-start = (bf16[33,32,128]{2,1,0:T(8,128)(2,1)S(1)}, bf16[33,32,128]{2,1,0:T(8,128)(2,1)S(1)}, u32[]{:S(2)}, u32[]{:S(2)}) collective-permute-start(bf16[33,32,128]{2,1,0:T(8,128)(2,1)S(1)} %get-tuple-element.15.refs_0_), channel_id=1, source_target_pairs={{0,1},{1,64},{64,65},{65,0},{2,3},{3,66},{66,67},{67,2},{4,5},{5,6... | collective-permute-start | bytes 811016 | tf_op jit(solution)/shard_map/ppermute | solution.py:243
  5.0 22.8 %collective-permute-start.1 = (bf16[33,32,128]{2,1,0:T(8,128)(2,1)S(1)}, bf16[33,32,128]{2,1,0:T(8,128)(2,1)S(1)}, u32[]{:S(2)}, u32[]{:S(2)}) collective-permute-start(bf16[33,32,128]{2,1,0:T(8,128)(2,1)S(1)} %get-tuple-element.15.refs_0_), channel_id=1, source_target_pairs={{0,65},{1,0},{64,1},{65,64},{2,67},{3,2},{66,3},{67,66},{4,69},{5,... | collective-permute-start | bytes 811016 | tf_op jit(solution)/shard_map/ppermute | solution.py:243
  7.2 20.6 %collective-permute-start.2 = (bf16[33,32,128]{2,1,0:T(8,128)(2,1)S(1)}, bf16[33,32,128]{2,1,0:T(8,128)(2,1)S(1)}, u32[]{:S(2)}, u32[]{:S(2)}) collective-permute-start(bf16[33,32,128]{2,1,0:T(8,128)(2,1)S(1)} %get-tuple-element.15.refs_0_), channel_id=1, source_target_pairs={{0,64},{1,65},{64,0},{65,1},{2,66},{3,67},{66,2},{67,3},{4,68},{5,... | collective-permute-start | bytes 811016 | tf_op jit(solution)/shard_map/ppermute | solution.py:243
  8.5 19.4 %all-to-all-start = ((s32[64,1,128]{2,1,0:T(1,128)}), s32[64,1,128]{2,1,0:T(1,128)S(1)}, u32[]{:S(2)}, u32[]{:S(2)}) async-start(s32[64,1,128]{2,1,0:T(1,128)} %bitcast.17), calls=%async_computation | async-start | bytes 65536 | tf_op jit(solution)/shard_map/all_to_all | solution.py:245
  18.6 10.4 %collective-permute-start.3 = (bf16[33,32,128]{2,1,0:T(8,128)(2,1)S(1)}, bf16[33,32,128]{2,1,0:T(8,128)(2,1)S(1)}, u32[]{:S(2)}, u32[]{:S(2)}) collective-permute-start(bf16[33,32,128]{2,1,0:T(8,128)(2,1)S(1)} %get-tuple-element.15.refs_0_), channel_id=1, source_target_pairs={{0,32},{32,0},{1,33},{33,1},{2,34},{34,2},{3,35},{35,3},{4,36},{36... | collective-permute-start | bytes 811016 | tf_op jit(solution)/shard_map/ppermute | solution.py:249
  27.9 1.9 %collective-permute-start.4 = (bf16[33,32,128]{2,1,0:T(8,128)(2,1)S(1)}, bf16[33,32,128]{2,1,0:T(8,128)(2,1)S(1)}, u32[]{:S(2)}, u32[]{:S(2)}) collective-permute-start(bf16[33,32,128]{2,1,0:T(8,128)(2,1)S(1)} %collective-permute-done.refs_1_), channel_id=1, source_target_pairs={{0,32},{32,0},{1,33},{33,1},{2,34},{34,2},{3,35},{35,3},{4,36},{36... | collective-permute-start | bytes 811016 | tf_op jit(solution)/shard_map/ppermute | solution.py:249
  28.6 1.6 %collective-permute-start.5 = (bf16[33,32,128]{2,1,0:T(8,128)(2,1)S(1)}, bf16[33,32,128]{2,1,0:T(8,128)(2,1)S(1)}, u32[]{:S(2)}, u32[]{:S(2)}) collective-permute-start(bf16[33,32,128]{2,1,0:T(8,128)(2,1)S(1)} %collective-permute-done.1.refs_2_), channel_id=1, source_target_pairs={{0,32},{32,0},{1,33},{33,1},{2,34},{34,2},{3,35},{35,3},{4,36},{36... | collective-permute-start | bytes 811016 | tf_op jit(solution)/shard_map/ppermute | solution.py:249
  28.7 1.9 %collective-permute-start.6 = (bf16[33,32,128]{2,1,0:T(8,128)(2,1)S(1)}, bf16[33,32,128]{2,1,0:T(8,128)(2,1)S(1)}, u32[]{:S(2)}, u32[]{:S(2)}) collective-permute-start(bf16[33,32,128]{2,1,0:T(8,128)(2,1)S(1)} %collective-permute-done.2.refs_3_), channel_id=1, source_target_pairs={{0,32},{32,0},{1,33},{33,1},{2,34},{34,2},{3,35},{35,3},{4,36},{36... | collective-permute-start | bytes 811016 | tf_op jit(solution)/shard_map/ppermute | solution.py:249
  43.9 20.2 %all-to-all-start.1 = ((bf16[16,8,8,512]{3,2,1,0:T(8,128)(2,1)}), bf16[16,8,8,512]{3,2,1,0:T(8,128)(2,1)S(1)}, u32[]{:S(2)}, u32[]{:S(2)}) async-start(bf16[16,8,8,512]{3,2,1,0:T(8,128)(2,1)} %stack_windows.1), calls=%async_computation.1 | async-start | bytes 2097152 | tf_op jit(solution)/shard_map/all_to_all | solution.py:272
  65.9 5.5 %collective-permute-start.7 = (bf16[16,1024]{1,0:T(8,128)(2,1)S(1)}, bf16[16,1024]{1,0:T(8,128)(2,1)S(1)}, u32[]{:S(2)}, u32[]{:S(2)}) collective-permute-start(bf16[16,1024]{1,0:T(8,128)(2,1)S(1)} %get-tuple-element.22), channel_id=1, source_target_pairs={{0,32},{32,0},{1,33},{33,1},{2,34},{34,2},{3,35},{35,3},{4,36},{36... | collective-permute-start | bytes 98312 | tf_op jit(solution)/shard_map/ppermute | solution.py:286
  68.2 4.3 %collective-permute-start.8 = (bf16[16,1024]{1,0:T(8,128)(2,1)S(1)}, bf16[16,1024]{1,0:T(8,128)(2,1)S(1)}, u32[]{:S(2)}, u32[]{:S(2)}) collective-permute-start(bf16[16,1024]{1,0:T(8,128)(2,1)S(1)} %get-tuple-element.23), channel_id=1, source_target_pairs={{0,64},{64,0},{1,65},{65,1},{2,66},{66,2},{3,67},{67,3},{4,68},{68... | collective-permute-start | bytes 98312 | tf_op jit(solution)/shard_map/ppermute | solution.py:287
  68.7 5.1 %collective-permute-start.9 = (bf16[16,1024]{1,0:T(8,128)(2,1)S(1)}, bf16[16,1024]{1,0:T(8,128)(2,1)S(1)}, u32[]{:S(2)}, u32[]{:S(2)}) collective-permute-start(bf16[16,1024]{1,0:T(8,128)(2,1)S(1)} %get-tuple-element.24), channel_id=1, source_target_pairs={{0,96},{32,64},{64,32},{96,0},{1,97},{33,65},{65,33},{97,1},{2,98}... | collective-permute-start | bytes 98312 | tf_op jit(solution)/shard_map/ppermute | solution.py:288

commit v2 on v1

--- a/solution.py
+++ b/solution.py
@@ -27,17 +27,20 @@
     groups = band_ref.shape[1] // offs
     spot = lax.broadcasted_iota(jnp.int32, (SUB, LANES), 1)
     line = lax.broadcasted_iota(jnp.int32, (SUB, LANES), 0)
-    here = (off_ref[0] * owned + (spot // groups)) * pitch
-    flags = jnp.full((SUB, LANES), (offs * owned * pitch) << CODE_SHIFT, jnp.int32)
+    here = jnp.zeros((SUB, LANES), jnp.int32)
+    first = jnp.zeros((SUB, LANES), jnp.int32)
+    count = 0
     for within in range(owned):
-        flags = jnp.where(spot == owned * groups + within, aperture_ref[0, within], flags)
-    first = jnp.zeros((SUB, LANES), jnp.int32)
-    for within in range(owned):
+        inside = aperture_ref[0, within]
+        turn = owned + inside * (count - owned)
+        count = count + inside
+        here = jnp.where(spot // groups == turn, (off_ref[0] * owned + within) * pitch, here)
         for group in range(groups):
             values = jnp.zeros((SUB, LANES), jnp.int32)
             for owner in range(offs):
                 values = jnp.where(line == owner, band_ref[within, owner * groups + group], values)
-            first = jnp.where(spot == within * groups + group, values, first)
+            first = jnp.where(spot == turn * groups + group, values, first)
+    flags = jnp.where(spot == owned * groups, count, (offs * owned * pitch) << CODE_SHIFT)
     code = ((here + (first >> 7)) << CODE_SHIFT) | ((-first) & (LANES - 1))
     block = jnp.where(spot < owned * groups, code, flags)
     tiles = meta_ref.shape[0] // offs
@@ -47,11 +50,18 @@
             meta_ref[owner * tiles + tile : owner * tiles + tile + SUB] = row
 
 
-def prepare_kernel(off_ref, assign_ref, band_ref, aperture_ref, raw_ref, out_ref, sent_ref, rows_ref, traces_ref, meta_ref, sems, *, offs, pitch):
-    fetch = pltpu.make_async_copy(raw_ref, traces_ref, sems.at[0])
-    fetch.start()
+def prepare_kernel(off_ref, *refs, offs, pitch):
+    *sources, out_ref, sent_ref, rows_ref, traces_ref, assign_ref, band_ref, aperture_ref, meta_ref, sems = refs
+    fetch, *smalls = [
+        pltpu.make_async_copy(source, held, sems.at[index])
+        for index, (source, held) in enumerate(zip(sources, (traces_ref, assign_ref, band_ref, aperture_ref)))
+    ]
+    for copy in (fetch, *smalls):
+        copy.start()
+    for copy in smalls:
+        copy.wait()
     code_rows(off_ref, band_ref, aperture_ref, meta_ref, offs=offs, owned=assign_ref.shape[1], pitch=pitch)
-    send = pltpu.make_async_copy(meta_ref, sent_ref, sems.at[1])
+    send = pltpu.make_async_copy(meta_ref, sent_ref, sems.at[4])
     send.start()
     fetch.wait()
     blocks, samples = traces_ref.shape
@@ -131,11 +141,11 @@
 
     def one_tile(tile, carry):
         count = 0
-        for block in range(blocks):
-            row = ((block // per_off) * tiles + tile) * LANES
-            within = block % per_off
-            list_ref[count] = row + within * groups
-            count = count + meta_ref[row + per_off * groups + within]
+        for owner in range(blocks // per_off):
+            row = (owner * tiles + tile) * LANES
+            for turn in range(per_off):
+                list_ref[count + turn] = row + turn * groups
+            count = count + meta_ref[row + per_off * groups]
         for more in range(TURNS[-1] - 1):
             list_ref[count + more] = per_off * groups + per_off
 
@@ -229,16 +239,19 @@
             pltpu.VMEM((blocks + 1, chunks, LANES), jnp.bfloat16),
             jax.ShapeDtypeStruct((offs * tiles, LANES), jnp.int32),
         ],
-        in_specs=[smem, smem, smem, smem, anywhere],
+        in_specs=[smem] + [anywhere] * 4,
         out_specs=[vmem, anywhere],
         scratch_shapes=[
             pltpu.VMEM((blocks * chunks, LANES), jnp.float32),
             pltpu.VMEM((blocks, samples), jnp.bfloat16),
+            pltpu.SMEM((assign.shape[2], per_off), jnp.int32),
+            pltpu.SMEM((per_off, all_groups), jnp.int32),
+            pltpu.SMEM((1, per_off), jnp.int32),
             pltpu.VMEM((offs * tiles, LANES), jnp.int32),
-            pltpu.SemaphoreType.DMA((2,)),
+            pltpu.SemaphoreType.DMA((5,)),
         ],
         name="prepare_traces",
-    )(off.reshape(1), jnp.transpose(assign[:, 0, :]), band, jnp.transpose(aperture), shot_traces[0, :, 0, :])
+    )(off.reshape(1), shot_traces[0, :, 0, :], jnp.transpose(assign[:, 0, :]), band, jnp.transpose(aperture))
     steps = (1, 3, 2)
     ring = [lax.ppermute(sent, ("zh", "zl"), ring_pairs(step)) for step in steps]
 

time: 74.2 us -> 73.4 us (0.989)
  Pallas kernels: 18.4 us -> 17.4 us
    pallas_call x1, Pallas kernels: 2.48 us -> 1.71 us  [local(): pl.pallas_call(functools.partial(prepare_kernel, offs=offs, pitch=pitch),...]
  transfers between devices with their start and end apart: 12 -> 12, of which waited for: 7 -> 7; matrix products, arithmetic and copies ran while one was open for 1% -> 2% of each run, Pallas kernels for 0% -> 0%
where the time goes in v2:
time: 73.4 us; the launch traced here: 73.6 us
  waiting for transfers between devices  27.9 us (38%)
  starting transfers between devices  27 us (37%)
  Pallas kernels  17.4 us (24%)
  local copies, waits for them, and re-layouts  1.12 us (2%)
    all_to_all x1, waiting for transfers between devices, local(): arrived = lax.all_to_all(stacked, PLANE, 0, 0, tiled=True)  15.4 us
    pallas_call x1, Pallas kernels, local(): pl.pallas_call(functools.partial(stack_kernel, pieces=len(pieces), blocks...  13.2 us
    all_to_all x1, starting transfers between devices, local(): meta = lax.all_to_all(row, OFF + PLANE, 0, 0, tiled=True)  10.2 us
    all_to_all x1, waiting for transfers between devices, local(): meta = lax.all_to_all(row, OFF + PLANE, 0, 0, tiled=True)  8.66 us
    ppermute x3, starting transfers between devices, local(): lax.ppermute(sent, ('zh', 'zl'), ring_pairs(step))  5.96 us
    all_to_all x1, starting transfers between devices, local(): arrived = lax.all_to_all(stacked, PLANE, 0, 0, tiled=True)  3.66 us
    ppermute x1, starting transfers between devices, local(): lax.ppermute(across, OFF, [(index, index ^ 3) for index in range(offs)])  2.75 us
    ppermute x1, starting transfers between devices, local(): beside = lax.ppermute(beside, 'core', swap)  2.22 us
  transfers between devices with their start and end apart: 12, of which 7 were waited for; matrix products, arithmetic and copies ran while one was open for 2% of the time, Pallas kernels for 0%

profile of v2, /device:TPU:1, one launch (start us, length us, event | category | flops | bytes accessed | tf_op | source)
XLA Modules:
  0.0 73.6 jit_solution(5602951442784562488)
XLA Ops:
  0.0 0.0 copy-start
  0.0 1.7 %prepare_traces.1 = (bf16[33,32,128]{2,1,0:T(8,128)(2,1)S(1)}, s32[64,128]{1,0:T(8,128)}) custom-call(s32[1]{0:T(128)} %bitcast.off_ref, bf16[32,4096]{1,0:T(8,128)(2,1)} %bitcast.16, s32[4,8]{1,0:T(4,128)} %bitcast.18, s32[8,32]{1,0:T(8,128)} %refs_2_.1, s32[1,8]{1,0:T(1,128)} %bitcast.19), custom_call_target="tpu_custom_call" | custom-call | tf_op jit(solution)/shard_map/prepare_traces/pallas_call | solution.py:236
  1.7 2.5 %collective-permute-start = (bf16[33,32,128]{2,1,0:T(8,128)(2,1)S(1)}, bf16[33,32,128]{2,1,0:T(8,128)(2,1)S(1)}, u32[]{:S(2)}, u32[]{:S(2)}) collective-permute-start(bf16[33,32,128]{2,1,0:T(8,128)(2,1)S(1)} %get-tuple-element.15.refs_0_), channel_id=1, source_target_pairs={{0,1},{1,64},{64,65},{65,0},{2,3},{3,66},{66,67},{67,2},{4,5},{5,6... | collective-permute-start | bytes 811016 | tf_op jit(solution)/shard_map/ppermute | solution.py:256
  4.3 2.2 %collective-permute-start.1 = (bf16[33,32,128]{2,1,0:T(8,128)(2,1)S(1)}, bf16[33,32,128]{2,1,0:T(8,128)(2,1)S(1)}, u32[]{:S(2)}, u32[]{:S(2)}) collective-permute-start(bf16[33,32,128]{2,1,0:T(8,128)(2,1)S(1)} %get-tuple-element.15.refs_0_), channel_id=1, source_target_pairs={{0,65},{1,0},{64,1},{65,64},{2,67},{3,2},{66,3},{67,66},{4,69},{5,... | collective-permute-start | bytes 811016 | tf_op jit(solution)/shard_map/ppermute | solution.py:256
  6.5 1.2 %collective-permute-start.2 = (bf16[33,32,128]{2,1,0:T(8,128)(2,1)S(1)}, bf16[33,32,128]{2,1,0:T(8,128)(2,1)S(1)}, u32[]{:S(2)}, u32[]{:S(2)}) collective-permute-start(bf16[33,32,128]{2,1,0:T(8,128)(2,1)S(1)} %get-tuple-element.15.refs_0_), channel_id=1, source_target_pairs={{0,64},{1,65},{64,0},{65,1},{2,66},{3,67},{66,2},{67,3},{4,68},{5,... | collective-permute-start | bytes 811016 | tf_op jit(solution)/shard_map/ppermute | solution.py:256
  7.7 10.2 %all-to-all-start = ((s32[64,1,128]{2,1,0:T(1,128)}), s32[64,1,128]{2,1,0:T(1,128)S(1)}, u32[]{:S(2)}, u32[]{:S(2)}) async-start(s32[64,1,128]{2,1,0:T(1,128)} %bitcast.17), calls=%async_computation | async-start | bytes 65536 | tf_op jit(solution)/shard_map/all_to_all | solution.py:258
  17.9 0.5 collective-permute-start.3
  18.4 8.7 %all-to-all-done = s32[64,1,128]{2,1,0:T(1,128)S(1)} async-done(((s32[64,1,128]{2,1,0:T(1,128)}), s32[64,1,128]{2,1,0:T(1,128)S(1)}, u32[]{:S(2)}, u32[]{:S(2)}) %all-to-all-start) | async-done | bytes 32800 | tf_op jit(solution)/shard_map/all_to_all | solution.py:258
  27.1 0.0 collective-permute-done.refs_1_
  27.1 0.0 collective-permute-done.1.refs_2_
  27.1 0.0 collective-permute-done.2.refs_3_
  27.1 0.7 collective-permute-start.4
  27.8 0.1 collective-permute-start.5
  27.9 0.4 collective-permute-start.6
  28.3 0.0 collective-permute-done.3.refs_4_
  28.3 0.7 collective-permute-done.4.refs_5_
  29.0 0.4 collective-permute-done.5.refs_6_
  29.4 0.4 collective-permute-done.6.refs_7_
  29.7 13.2 %stack_windows.1 = bf16[16,8,8,512]{3,2,1,0:T(8,128)(2,1)} custom-call(s32[1]{0:T(128)} %bitcast.1.z_ref, s32[1]{0:T(128)} %bitcast.2.core_ref, s32[8192]{0:T(1024)S(1)} %bitcast.15, bf16[33,32,128]{2,1,0:T(8,128)(2,1)S(1)} %get-tuple-element.15.refs_0_, bf16[33,32,128]{2,1,0:T(8,128)(2,1)S(1)} %collective-permute-done.refs_1_, ...), custom_call_target="tpu_custom_call" | custom-call | tf_op jit(solution)/shard_map/stack_windows/pallas_call | solution.py:263
  42.9 3.7 %all-to-all-start.1 = ((bf16[16,8,8,512]{3,2,1,0:T(8,128)(2,1)}), bf16[16,8,8,512]{3,2,1,0:T(8,128)(2,1)S(1)}, u32[]{:S(2)}, u32[]{:S(2)}) async-start(bf16[16,8,8,512]{3,2,1,0:T(8,128)(2,1)} %stack_windows.1), calls=%async_computation.1 | async-start | bytes 2097152 | tf_op jit(solution)/shard_map/all_to_all | solution.py:285
  46.6 0.0 copy-done
  46.6 1.1 %dynamic-slice_bitcast_fusion.interp_ref = bf16[8,64,512]{2,1,0:T(8,128)(2,1)S(1)} fusion(bf16[32,512,64]{1,2,0:T(8,128)(2,1)} %param.10, s32[]{:T(128)S(6)} %select_n.4), kind=kLoop, calls=%fused_computation | loop fusion | bytes 1048580 | tf_op jit(solution)/shard_map/dynamic_slice | solution.py:287
  47.7 15.4 %all-to-all-done.1.stacked_ref = bf16[16,8,8,512]{3,2,1,0:T(8,128)(2,1)S(1)} async-done(((bf16[16,8,8,512]{3,2,1,0:T(8,128)(2,1)}), bf16[16,8,8,512]{3,2,1,0:T(8,128)(2,1)S(1)}, u32[]{:S(2)}, u32[]{:S(2)}) %all-to-all-start.1) | async-done | bytes 1048608 | tf_op jit(solution)/shard_map/all_to_all | solution.py:285
  63.2 1.8 %image_groups.1 = (f32[16,1024]{1,0:T(8,128)S(1)}, bf16[16,1024]{1,0:T(8,128)(2,1)S(1)}, bf16[16,1024]{1,0:T(8,128)(2,1)S(1)}, bf16[16,1024]{1,0:T(8,128)(2,1)S(1)}) custom-call(s32[1]{0:T(128)} %bitcast.off_ref, bf16[16,8,8,512]{3,2,1,0:T(8,128)(2,1)S(1)} %all-to-all-done.1.stacked_ref, bf16[8,64,512]{2,1,0:T(8,128)(2,1)S(1)} %dynamic-slice_bitcast_fusion.interp_ref, ...), custom_call_target="tpu_custom_call" | custom-call | tf_op jit(solution)/shard_map/image_groups/pallas_call | solution.py:290
  65.0 2.2 %collective-permute-start.7 = (bf16[16,1024]{1,0:T(8,128)(2,1)S(1)}, bf16[16,1024]{1,0:T(8,128)(2,1)S(1)}, u32[]{:S(2)}, u32[]{:S(2)}) collective-permute-start(bf16[16,1024]{1,0:T(8,128)(2,1)S(1)} %get-tuple-element.22), channel_id=1, source_target_pairs={{0,32},{32,0},{1,33},{33,1},{2,34},{34,2},{3,35},{35,3},{4,36},{36... | collective-permute-start | bytes 98312 | tf_op jit(solution)/shard_map/ppermute | solution.py:299
  67.2 0.5 collective-permute-start.8
  67.7 2.7 %collective-permute-start.9 = (bf16[16,1024]{1,0:T(8,128)(2,1)S(1)}, bf16[16,1024]{1,0:T(8,128)(2,1)S(1)}, u32[]{:S(2)}, u32[]{:S(2)}) collective-permute-start(bf16[16,1024]{1,0:T(8,128)(2,1)S(1)} %get-tuple-element.24), channel_id=1, source_target_pairs={{0,96},{32,64},{64,32},{96,0},{1,97},{33,65},{65,33},{97,1},{2,98}... | collective-permute-start | bytes 98312 | tf_op jit(solution)/shard_map/ppermute | solution.py:301
  70.4 0.0 collective-permute-done.7.refs_1_
  70.4 1.1 %collective-permute-done.8.refs_2_ = bf16[16,1024]{1,0:T(8,128)(2,1)S(1)} collective-permute-done((bf16[16,1024]{1,0:T(8,128)(2,1)S(1)}, bf16[16,1024]{1,0:T(8,128)(2,1)S(1)}, u32[]{:S(2)}, u32[]{:S(2)}) %collective-permute-start.8) | collective-permute-done | bytes 32800 | tf_op jit(solution)/shard_map/ppermute | solution.py:300
  71.5 1.4 %collective-permute-done.9.refs_3_ = bf16[16,1024]{1,0:T(8,128)(2,1)S(1)} collective-permute-done((bf16[16,1024]{1,0:T(8,128)(2,1)S(1)}, bf16[16,1024]{1,0:T(8,128)(2,1)S(1)}, u32[]{:S(2)}, u32[]{:S(2)}) %collective-permute-start.9) | collective-permute-done | bytes 32800 | tf_op jit(solution)/shard_map/ppermute | solution.py:301
  72.8 0.7 join_groups.1
  (1 shorter events, 0.0 us)
Async XLA Ops:
  0.0 46.6 %copy-start = (bf16[32,128,128]{2,1,0:T(8,128)(2,1)S(1)}, bf16[32,128,128]{2,1,0:T(8,128)(2,1)}, u32[]{:S(2)}) copy-start(bf16[32,128,128]{2,1,0:T(8,128)(2,1)} %param.11) | copy-start | bytes 3145732
  1.7 25.4 %collective-permute-start = (bf16[33,32,128]{2,1,0:T(8,128)(2,1)S(1)}, bf16[33,32,128]{2,1,0:T(8,128)(2,1)S(1)}, u32[]{:S(2)}, u32[]{:S(2)}) collective-permute-start(bf16[33,32,128]{2,1,0:T(8,128)(2,1)S(1)} %get-tuple-element.15.refs_0_), channel_id=1, source_target_pairs={{0,1},{1,64},{64,65},{65,0},{2,3},{3,66},{66,67},{67,2},{4,5},{5,6... | collective-permute-start | bytes 811016 | tf_op jit(solution)/shard_map/ppermute | solution.py:256
  4.3 22.8 %collective-permute-start.1 = (bf16[33,32,128]{2,1,0:T(8,128)(2,1)S(1)}, bf16[33,32,128]{2,1,0:T(8,128)(2,1)S(1)}, u32[]{:S(2)}, u32[]{:S(2)}) collective-permute-start(bf16[33,32,128]{2,1,0:T(8,128)(2,1)S(1)} %get-tuple-element.15.refs_0_), channel_id=1, source_target_pairs={{0,65},{1,0},{64,1},{65,64},{2,67},{3,2},{66,3},{67,66},{4,69},{5,... | collective-permute-start | bytes 811016 | tf_op jit(solution)/shard_map/ppermute | solution.py:256
  6.5 20.6 %collective-permute-start.2 = (bf16[33,32,128]{2,1,0:T(8,128)(2,1)S(1)}, bf16[33,32,128]{2,1,0:T(8,128)(2,1)S(1)}, u32[]{:S(2)}, u32[]{:S(2)}) collective-permute-start(bf16[33,32,128]{2,1,0:T(8,128)(2,1)S(1)} %get-tuple-element.15.refs_0_), channel_id=1, source_target_pairs={{0,64},{1,65},{64,0},{65,1},{2,66},{3,67},{66,2},{67,3},{4,68},{5,... | collective-permute-start | bytes 811016 | tf_op jit(solution)/shard_map/ppermute | solution.py:256
  7.7 19.4 %all-to-all-start = ((s32[64,1,128]{2,1,0:T(1,128)}), s32[64,1,128]{2,1,0:T(1,128)S(1)}, u32[]{:S(2)}, u32[]{:S(2)}) async-start(s32[64,1,128]{2,1,0:T(1,128)} %bitcast.17), calls=%async_computation | async-start | bytes 65536 | tf_op jit(solution)/shard_map/all_to_all | solution.py:258
  17.9 10.4 %collective-permute-start.3 = (bf16[33,32,128]{2,1,0:T(8,128)(2,1)S(1)}, bf16[33,32,128]{2,1,0:T(8,128)(2,1)S(1)}, u32[]{:S(2)}, u32[]{:S(2)}) collective-permute-start(bf16[33,32,128]{2,1,0:T(8,128)(2,1)S(1)} %get-tuple-element.15.refs_0_), channel_id=1, source_target_pairs={{0,32},{32,0},{1,33},{33,1},{2,34},{34,2},{3,35},{35,3},{4,36},{36... | collective-permute-start | bytes 811016 | tf_op jit(solution)/shard_map/ppermute | solution.py:262
  27.1 1.9 %collective-permute-start.4 = (bf16[33,32,128]{2,1,0:T(8,128)(2,1)S(1)}, bf16[33,32,128]{2,1,0:T(8,128)(2,1)S(1)}, u32[]{:S(2)}, u32[]{:S(2)}) collective-permute-start(bf16[33,32,128]{2,1,0:T(8,128)(2,1)S(1)} %collective-permute-done.refs_1_), channel_id=1, source_target_pairs={{0,32},{32,0},{1,33},{33,1},{2,34},{34,2},{3,35},{35,3},{4,36},{36... | collective-permute-start | bytes 811016 | tf_op jit(solution)/shard_map/ppermute | solution.py:262
  27.8 1.6 %collective-permute-start.5 = (bf16[33,32,128]{2,1,0:T(8,128)(2,1)S(1)}, bf16[33,32,128]{2,1,0:T(8,128)(2,1)S(1)}, u32[]{:S(2)}, u32[]{:S(2)}) collective-permute-start(bf16[33,32,128]{2,1,0:T(8,128)(2,1)S(1)} %collective-permute-done.1.refs_2_), channel_id=1, source_target_pairs={{0,32},{32,0},{1,33},{33,1},{2,34},{34,2},{3,35},{35,3},{4,36},{36... | collective-permute-start | bytes 811016 | tf_op jit(solution)/shard_map/ppermute | solution.py:262
  27.9 1.9 %collective-permute-start.6 = (bf16[33,32,128]{2,1,0:T(8,128)(2,1)S(1)}, bf16[33,32,128]{2,1,0:T(8,128)(2,1)S(1)}, u32[]{:S(2)}, u32[]{:S(2)}) collective-permute-start(bf16[33,32,128]{2,1,0:T(8,128)(2,1)S(1)} %collective-permute-done.2.refs_3_), channel_id=1, source_target_pairs={{0,32},{32,0},{1,33},{33,1},{2,34},{34,2},{3,35},{35,3},{4,36},{36... | collective-permute-start | bytes 811016 | tf_op jit(solution)/shard_map/ppermute | solution.py:262
  42.9 20.2 %all-to-all-start.1 = ((bf16[16,8,8,512]{3,2,1,0:T(8,128)(2,1)}), bf16[16,8,8,512]{3,2,1,0:T(8,128)(2,1)S(1)}, u32[]{:S(2)}, u32[]{:S(2)}) async-start(bf16[16,8,8,512]{3,2,1,0:T(8,128)(2,1)} %stack_windows.1), calls=%async_computation.1 | async-start | bytes 2097152 | tf_op jit(solution)/shard_map/all_to_all | solution.py:285
  65.0 5.5 %collective-permute-start.7 = (bf16[16,1024]{1,0:T(8,128)(2,1)S(1)}, bf16[16,1024]{1,0:T(8,128)(2,1)S(1)}, u32[]{:S(2)}, u32[]{:S(2)}) collective-permute-start(bf16[16,1024]{1,0:T(8,128)(2,1)S(1)} %get-tuple-element.22), channel_id=1, source_target_pairs={{0,32},{32,0},{1,33},{33,1},{2,34},{34,2},{3,35},{35,3},{4,36},{36... | collective-permute-start | bytes 98312 | tf_op jit(solution)/shard_map/ppermute | solution.py:299
  67.2 4.3 %collective-permute-start.8 = (bf16[16,1024]{1,0:T(8,128)(2,1)S(1)}, bf16[16,1024]{1,0:T(8,128)(2,1)S(1)}, u32[]{:S(2)}, u32[]{:S(2)}) collective-permute-start(bf16[16,1024]{1,0:T(8,128)(2,1)S(1)} %get-tuple-element.23), channel_id=1, source_target_pairs={{0,64},{64,0},{1,65},{65,1},{2,66},{66,2},{3,67},{67,3},{4,68},{68... | collective-permute-start | bytes 98312 | tf_op jit(solution)/shard_map/ppermute | solution.py:300
  67.7 5.2 %collective-permute-start.9 = (bf16[16,1024]{1,0:T(8,128)(2,1)S(1)}, bf16[16,1024]{1,0:T(8,128)(2,1)S(1)}, u32[]{:S(2)}, u32[]{:S(2)}) collective-permute-start(bf16[16,1024]{1,0:T(8,128)(2,1)S(1)} %get-tuple-element.24), channel_id=1, source_target_pairs={{0,96},{32,64},{64,32},{96,0},{1,97},{33,65},{65,33},{97,1},{2,98}... | collective-permute-start | bytes 98312 | tf_op jit(solution)/shard_map/ppermute | solution.py:301

commit v3 on v2

--- a/solution.py
+++ b/solution.py
@@ -17,6 +17,11 @@
 CODE_SHIFT = 7
 TURNS = (16, 8)
 MASK = jnp.int16
+VMEM_BYTES = 24 * 2**20
+
+
+def in_hbm(array):
+    return pltpu.with_memory_space_constraint(array, pltpu.HBM)
 
 
 def in_vmem(array):
@@ -44,10 +49,10 @@
     code = ((here + (first >> 7)) << CODE_SHIFT) | ((-first) & (LANES - 1))
     block = jnp.where(spot < owned * groups, code, flags)
     tiles = meta_ref.shape[0] // offs
-    for owner in range(offs):
-        row = jnp.broadcast_to(block[owner : owner + 1], (SUB, LANES))
-        for tile in range(0, tiles, SUB):
-            meta_ref[owner * tiles + tile : owner * tiles + tile + SUB] = row
+    for core in range(2):
+        row = jnp.where(line % 2 == 0, block[core : core + 1], block[2 + core : 3 + core])
+        for start in range(0, 2 * tiles, SUB):
+            meta_ref[core * 2 * tiles + start : core * 2 * tiles + start + SUB] = row
 
 
 def prepare_kernel(off_ref, *refs, offs, pitch):
@@ -90,11 +95,9 @@
     return (from_z >> 1) * 4 + (core ^ (piece // 4)) * 2 + (from_z & 1)
 
 
-def stack_kernel(z_ref, core_ref, table_ref, *refs, pieces, blocks, chunks, per_off, tiles, groups, window):
+def place_kernel(z_ref, core_ref, *refs, pieces, blocks, chunks, per_off, tiles, groups, window):
     piece_refs = refs[:pieces]
-    out_ref, sums_ref, traces_ref, rows_ref, pairs_ref, words_ref, codes_ref, meta_ref, list_ref, sems, out_sems = refs[pieces:]
-    table = pltpu.make_async_copy(table_ref, meta_ref, sems.at[pieces + 1])
-    table.start()
+    pairs_ref, traces_ref, rows_ref, words_ref, codes_ref, sems = refs[pieces:]
     slots = SUB
     parts = window // LANES
     halves = parts // 2
@@ -137,12 +140,29 @@
         return carry
 
     lax.fori_loop(0, blocks // per_off, place, 0)
-    table.wait()
+
+
+def stack_kernel(z_ref, near_ref, far_ref, pairs_ref, out_ref, sums_ref, meta_ref, list_ref, sems, out_sems, *, blocks, chunks, per_off, tiles, groups, window):
+    z = z_ref[0]
+    span = near_ref.shape[0]
+    fetches = [
+        pltpu.make_async_copy(ref, meta_ref.at[pl.ds(index * span, span)], sems.at[index])
+        for index, ref in enumerate((near_ref, far_ref))
+    ]
+    for table in fetches:
+        table.start()
+    slots = SUB
+    parts = window // LANES
+    halves = parts // 2
+    pitch = chunks - halves + 1
+    lane = lax.broadcasted_iota(jnp.int32, (2 * slots, LANES), 1).astype(MASK)
+    for table in fetches:
+        table.wait()
 
     def one_tile(tile, carry):
         count = 0
         for owner in range(blocks // per_off):
-            row = (owner * tiles + tile) * LANES
+            row = owner // 2 * span + ((owner % 2 * tiles + tile) * 2 + (z >> 1)) * LANES
             for turn in range(per_off):
                 list_ref[count + turn] = row + turn * groups
             count = count + meta_ref[row + per_off * groups]
@@ -251,36 +271,48 @@
             pltpu.SemaphoreType.DMA((5,)),
         ],
         name="prepare_traces",
-    )(off.reshape(1), shot_traces[0, :, 0, :], jnp.transpose(assign[:, 0, :]), band, jnp.transpose(aperture))
+    )(off.reshape(1), *map(in_hbm, (shot_traces[0, :, 0, :], jnp.transpose(assign[:, 0, :]), band, jnp.transpose(aperture))))
     steps = (1, 3, 2)
     ring = [lax.ppermute(sent, ("zh", "zl"), ring_pairs(step)) for step in steps]
 
-    meta = lax.all_to_all(row, OFF + PLANE, 0, 0, tiled=True)
+    meta = lax.all_to_all(row, ("core",) + PLANE, 0, 0, tiled=True)
 
     *ring, meta = lax.optimization_barrier((*ring, meta))
     column = [sent, *ring]
     pieces = column + [lax.ppermute(piece, "core", swap) for piece in column]
+    tables = [meta.reshape(-1), lax.ppermute(meta, "zh", swap).reshape(-1)]
+    pairs = pl.pallas_call(
+        functools.partial(
+            place_kernel, pieces=len(pieces), blocks=blocks, chunks=chunks, per_off=per_off, tiles=tiles, groups=groups, window=window
+        ),
+        out_shape=pltpu.VMEM(((blocks + 1) * pitch, 2 * SUB, LANES), jnp.bfloat16),
+        in_specs=[smem, smem] + [vmem] * len(pieces),
+        out_specs=vmem,
+        scratch_shapes=[
+            pltpu.VMEM((len(pieces), blocks + 1, chunks, LANES), jnp.bfloat16),
+            pltpu.VMEM((2, (chunks + 1) * SUB, LANES), jnp.float32),
+            pltpu.VMEM((len(pieces), LANES), jnp.int32),
+            pltpu.SMEM((len(pieces), LANES), jnp.int32),
+            pltpu.SemaphoreType.DMA((len(pieces) + 1,)),
+        ],
+        compiler_params=pltpu.CompilerParams(vmem_limit_bytes=VMEM_BYTES),
+        name="place_traces",
+    )(z.reshape(1), core.reshape(1), *map(in_vmem, pieces))
     stacked = pl.pallas_call(
-        functools.partial(
-            stack_kernel, pieces=len(pieces), blocks=blocks, chunks=chunks, per_off=per_off, tiles=tiles, groups=groups, window=window
-        ),
+        functools.partial(stack_kernel, blocks=blocks, chunks=chunks, per_off=per_off, tiles=tiles, groups=groups, window=window),
         out_shape=jax.ShapeDtypeStruct((tiles, groups, SUB, window), jnp.bfloat16),
-        in_specs=[smem, smem, anywhere] + [vmem] * len(pieces),
+        in_specs=[smem, anywhere, anywhere, vmem],
         out_specs=anywhere,
         scratch_shapes=[
             pltpu.VMEM((tiles, groups, SUB, window), jnp.bfloat16),
-            pltpu.VMEM((len(pieces), blocks + 1, chunks, LANES), jnp.bfloat16),
-            pltpu.VMEM((2, (chunks + 1) * SUB, LANES), jnp.float32),
-            pltpu.VMEM(((blocks + 1) * pitch, 2 * SUB, LANES), jnp.bfloat16),
-            pltpu.VMEM((len(pieces), LANES), jnp.int32),
-            pltpu.SMEM((len(pieces), LANES), jnp.int32),
-            pltpu.SMEM((offs * tiles * LANES,), jnp.int32),
+            pltpu.SMEM((2 * offs * tiles * LANES,), jnp.int32),
             pltpu.SMEM((blocks + TURNS[-1] - 1,), jnp.int32),
-            pltpu.SemaphoreType.DMA((len(pieces) + 2,)),
+            pltpu.SemaphoreType.DMA((2,)),
             pltpu.SemaphoreType.DMA((tiles,)),
         ],
+        compiler_params=pltpu.CompilerParams(vmem_limit_bytes=VMEM_BYTES),
         name="stack_windows",
-    )(z.reshape(1), core.reshape(1), in_vmem(meta.reshape(-1)), *map(in_vmem, pieces))
+    )(z.reshape(1), *map(in_vmem, tables), in_vmem(pairs))
 
     arrived = lax.all_to_all(stacked, PLANE, 0, 0, tiled=True)
 
@@ -296,9 +328,10 @@
         name="image_groups",
     )(off.reshape(1), in_vmem(arrived), in_vmem(interp_here), in_vmem(amp_here))
 
-    beside = lax.ppermute(beside, "core", swap)
-    far = lax.ppermute(far, "zh", swap)
-    across = lax.ppermute(across, OFF, [(index, index ^ 3) for index in range(offs)])
+    far, across, beside = (
+        lax.ppermute(strip, OFF, [(index, index ^ apart) for index in range(offs)])
+        for apart, strip in ((2, far), (3, across), (1, beside))
+    )
     return pl.pallas_call(
         join_kernel,
         out_shape=jax.ShapeDtypeStruct((depth // offs, offs * groups * pixels), jnp.float32),

time: 73.4 us -> 70.7 us (0.963); the launches traced: 73.6 us -> 69.8 us
  waiting for transfers between devices: 27.9 us -> 24.6 us
    ppermute x3 -> x4, starting transfers between devices: 5.45 us -> 7.55 us  [the longest x3 6.07 us: local(): lax.ppermute(strip, OFF, [(index, index ^ apart) for index in range(offs)])]
    all_to_all x1, waiting for transfers between devices: 8.66 us -> 6.69 us  [local(): meta = lax.all_to_all(row, ('core',) + PLANE, 0, 0, tiled=True)]
    all_to_all x1, starting transfers between devices: 10.2 us -> 8.6 us  [local(): meta = lax.all_to_all(row, ('core',) + PLANE, 0, 0, tiled=True)]
    ppermute x4, waiting for transfers between devices: 1.43 us -> 0.01 us  [local(): pieces = column + [lax.ppermute(piece, 'core', swap) for piece in column]]
    ppermute x3 -> x4, waiting for transfers between devices: 2.41 us -> 3.8 us  [the longest x3 2.85 us: local(): lax.ppermute(strip, OFF, [(index, index ^ apart) for index in range(offs)])]
    all_to_all x1, waiting for transfers between devices: 15.4 us -> 14.1 us  [local(): arrived = lax.all_to_all(stacked, PLANE, 0, 0, tiled=True)]
    pallas_call x1 -> x2, Pallas kernels: 13.2 us -> 12.5 us  [the longest x1 10.6 us: local(): pl.pallas_call(functools.partial(stack_kernel, blocks=blocks, chunks=chun...]
  transfers between devices with their start and end apart: 12 -> 13, of which waited for: 7 -> 5; matrix products, arithmetic and copies ran while one was open for 2% -> 2% of each run, Pallas kernels for 0% -> 3%
where the time goes in v3:
time: 70.7 us; the launch traced here: 69.8 us
  starting transfers between devices  27.3 us (39%)
  waiting for transfers between devices  24.6 us (35%)
  Pallas kernels  16.7 us (24%)
  local copies, waits for them, and re-layouts  1.12 us (2%)
    all_to_all x1, waiting for transfers between devices, local(): arrived = lax.all_to_all(stacked, PLANE, 0, 0, tiled=True)  14.1 us
    pallas_call x1, Pallas kernels, local(): pl.pallas_call(functools.partial(stack_kernel, blocks=blocks, chunks=chun...  10.6 us
    all_to_all x1, starting transfers between devices, local(): meta = lax.all_to_all(row, ('core',) + PLANE, 0, 0, tiled=True)  8.6 us
    all_to_all x1, waiting for transfers between devices, local(): meta = lax.all_to_all(row, ('core',) + PLANE, 0, 0, tiled=True)  6.69 us
    ppermute x3, starting transfers between devices, local(): lax.ppermute(strip, OFF, [(index, index ^ apart) for index in range(offs)])  6.07 us
    ppermute x3, starting transfers between devices, local(): lax.ppermute(sent, ('zh', 'zl'), ring_pairs(step))  5.96 us
    all_to_all x1, starting transfers between devices, local(): arrived = lax.all_to_all(stacked, PLANE, 0, 0, tiled=True)  3.66 us
    ppermute x3, waiting for transfers between devices, local(): lax.ppermute(strip, OFF, [(index, index ^ apart) for index in range(offs)])  2.85 us
  transfers between devices with their start and end apart: 13, of which 5 were waited for; matrix products, arithmetic and copies ran while one was open for 2% of the time, Pallas kernels for 3%

profile of v3, /device:TPU:1, one launch (start us, length us, event | category | flops | bytes accessed | tf_op | source)
XLA Modules:
  0.0 69.8 jit_solution(16951554999655972008)
XLA Ops:
  0.0 0.0 copy-start
  0.0 1.7 %prepare_traces.1 = (bf16[33,32,128]{2,1,0:T(8,128)(2,1)S(1)}, s32[64,128]{1,0:T(8,128)}) custom-call(s32[1]{0:T(128)} %bitcast.off_ref, bf16[32,4096]{1,0:T(8,128)(2,1)} %bitcast.17, s32[4,8]{1,0:T(4,128)} %bitcast.19, s32[8,32]{1,0:T(8,128)} %refs_2_.1, s32[1,8]{1,0:T(1,128)} %bitcast.20), custom_call_target="tpu_custom_call" | custom-call | tf_op jit(solution)/shard_map/prepare_traces/pallas_call | solution.py:256
  1.7 2.5 %collective-permute-start = (bf16[33,32,128]{2,1,0:T(8,128)(2,1)S(1)}, bf16[33,32,128]{2,1,0:T(8,128)(2,1)S(1)}, u32[]{:S(2)}, u32[]{:S(2)}) collective-permute-start(bf16[33,32,128]{2,1,0:T(8,128)(2,1)S(1)} %get-tuple-element.15.refs_0_), channel_id=1, source_target_pairs={{0,1},{1,64},{64,65},{65,0},{2,3},{3,66},{66,67},{67,2},{4,5},{5,6... | collective-permute-start | bytes 811016 | tf_op jit(solution)/shard_map/ppermute | solution.py:276
  4.3 2.2 %collective-permute-start.1 = (bf16[33,32,128]{2,1,0:T(8,128)(2,1)S(1)}, bf16[33,32,128]{2,1,0:T(8,128)(2,1)S(1)}, u32[]{:S(2)}, u32[]{:S(2)}) collective-permute-start(bf16[33,32,128]{2,1,0:T(8,128)(2,1)S(1)} %get-tuple-element.15.refs_0_), channel_id=1, source_target_pairs={{0,65},{1,0},{64,1},{65,64},{2,67},{3,2},{66,3},{67,66},{4,69},{5,... | collective-permute-start | bytes 811016 | tf_op jit(solution)/shard_map/ppermute | solution.py:276
  6.5 1.2 %collective-permute-start.2 = (bf16[33,32,128]{2,1,0:T(8,128)(2,1)S(1)}, bf16[33,32,128]{2,1,0:T(8,128)(2,1)S(1)}, u32[]{:S(2)}, u32[]{:S(2)}) collective-permute-start(bf16[33,32,128]{2,1,0:T(8,128)(2,1)S(1)} %get-tuple-element.15.refs_0_), channel_id=1, source_target_pairs={{0,64},{1,65},{64,0},{65,1},{2,66},{3,67},{66,2},{67,3},{4,68},{5,... | collective-permute-start | bytes 811016 | tf_op jit(solution)/shard_map/ppermute | solution.py:276
  7.7 8.6 %all-to-all-start = ((s32[32,2,128]{2,1,0:T(2,128)}), s32[32,2,128]{2,1,0:T(2,128)S(1)}, u32[]{:S(2)}, u32[]{:S(2)}) async-start(s32[32,2,128]{2,1,0:T(2,128)} %bitcast.18), calls=%async_computation | async-start | bytes 65536 | tf_op jit(solution)/shard_map/all_to_all | solution.py:278
  16.3 0.3 collective-permute-start.4
  16.6 6.7 %all-to-all-done = s32[32,2,128]{2,1,0:T(2,128)S(1)} async-done(((s32[32,2,128]{2,1,0:T(2,128)}), s32[32,2,128]{2,1,0:T(2,128)S(1)}, u32[]{:S(2)}, u32[]{:S(2)}) %all-to-all-start) | async-done | bytes 32800 | tf_op jit(solution)/shard_map/all_to_all | solution.py:278
  23.3 0.0 collective-permute-done.refs_1_
  23.3 0.0 collective-permute-done.1.refs_2_
  23.3 0.0 collective-permute-done.2.refs_3_
  23.3 0.7 collective-permute-start.5
  24.0 0.1 collective-permute-start.6
  24.1 0.4 collective-permute-start.7
  24.5 1.5 %collective-permute-start.3 = (s32[64,128]{1,0:T(8,128)S(1)}, s32[64,128]{1,0:T(8,128)S(1)}, u32[]{:S(2)}, u32[]{:S(2)}) collective-permute-start(s32[64,128]{1,0:T(8,128)S(1)} %bitcast.14), channel_id=1, source_target_pairs={{0,64},{64,0},{1,65},{65,1},{2,66},{66,2},{3,67},{67,3},{4,68},{68... | collective-permute-start | bytes 98312 | tf_op jit(solution)/shard_map/ppermute | solution.py:283
  26.0 0.0 collective-permute-done.4.refs_4_
  26.0 0.0 collective-permute-done.5.refs_5_
  26.0 0.0 collective-permute-done.6.refs_6_
  26.0 0.0 collective-permute-done.7.refs_7_
  26.0 1.8 %place_traces.1.pairs_ref = bf16[1023,16,128]{2,1,0:T(8,128)(2,1)S(1)} custom-call(s32[1]{0:T(128)} %bitcast.1.z_ref, s32[1]{0:T(128)} %bitcast.10.core_ref, bf16[33,32,128]{2,1,0:T(8,128)(2,1)S(1)} %get-tuple-element.15.refs_0_, bf16[33,32,128]{2,1,0:T(8,128)(2,1)S(1)} %collective-permute-done.refs_1_, ...), custom_call_target="tpu_custom_call" | custom-call | tf_op jit(solution)/shard_map/place_traces/pallas_call | solution.py:284
  27.9 0.9 %collective-permute-done.3 = s32[64,128]{1,0:T(8,128)S(1)} collective-permute-done((s32[64,128]{1,0:T(8,128)S(1)}, s32[64,128]{1,0:T(8,128)S(1)}, u32[]{:S(2)}, u32[]{:S(2)}) %collective-permute-start.3) | collective-permute-done | bytes 32800 | tf_op jit(solution)/shard_map/ppermute | solution.py:283
  28.8 10.6 %stack_windows.1 = bf16[16,8,8,512]{3,2,1,0:T(8,128)(2,1)} custom-call(s32[1]{0:T(128)} %bitcast.1.z_ref, s32[8192]{0:T(1024)S(1)} %bitcast.15, s32[8192]{0:T(1024)S(1)} %bitcast.16, bf16[1023,16,128]{2,1,0:T(8,128)(2,1)S(1)} %place_traces.1.pairs_ref), custom_call_target="tpu_custom_call" | custom-call | tf_op jit(solution)/shard_map/stack_windows/pallas_call | solution.py:301
  39.5 3.7 %all-to-all-start.1 = ((bf16[16,8,8,512]{3,2,1,0:T(8,128)(2,1)}), bf16[16,8,8,512]{3,2,1,0:T(8,128)(2,1)S(1)}, u32[]{:S(2)}, u32[]{:S(2)}) async-start(bf16[16,8,8,512]{3,2,1,0:T(8,128)(2,1)} %stack_windows.1), calls=%async_computation.1 | async-start | bytes 2097152 | tf_op jit(solution)/shard_map/all_to_all | solution.py:317
  43.1 0.0 copy-done
  43.2 1.1 %dynamic-slice_bitcast_fusion.interp_ref = bf16[8,64,512]{2,1,0:T(8,128)(2,1)S(1)} fusion(bf16[32,512,64]{1,2,0:T(8,128)(2,1)} %param.10, s32[]{:T(128)S(6)} %select_n.4), kind=kLoop, calls=%fused_computation | loop fusion | bytes 1048580 | tf_op jit(solution)/shard_map/dynamic_slice | solution.py:319
  44.3 14.1 %all-to-all-done.1.stacked_ref = bf16[16,8,8,512]{3,2,1,0:T(8,128)(2,1)S(1)} async-done(((bf16[16,8,8,512]{3,2,1,0:T(8,128)(2,1)}), bf16[16,8,8,512]{3,2,1,0:T(8,128)(2,1)S(1)}, u32[]{:S(2)}, u32[]{:S(2)}) %all-to-all-start.1) | async-done | bytes 1048608 | tf_op jit(solution)/shard_map/all_to_all | solution.py:317
  58.4 1.8 %image_groups.1 = (f32[16,1024]{1,0:T(8,128)S(1)}, bf16[16,1024]{1,0:T(8,128)(2,1)S(1)}, bf16[16,1024]{1,0:T(8,128)(2,1)S(1)}, bf16[16,1024]{1,0:T(8,128)(2,1)S(1)}) custom-call(s32[1]{0:T(128)} %bitcast.off_ref, bf16[16,8,8,512]{3,2,1,0:T(8,128)(2,1)S(1)} %all-to-all-done.1.stacked_ref, bf16[8,64,512]{2,1,0:T(8,128)(2,1)S(1)} %dynamic-slice_bitcast_fusion.interp_ref, ...), custom_call_target="tpu_custom_call" | custom-call | tf_op jit(solution)/shard_map/image_groups/pallas_call | solution.py:322
  60.2 4.7 %collective-permute-start.10 = (bf16[16,1024]{1,0:T(8,128)(2,1)S(1)}, bf16[16,1024]{1,0:T(8,128)(2,1)S(1)}, u32[]{:S(2)}, u32[]{:S(2)}) collective-permute-start(bf16[16,1024]{1,0:T(8,128)(2,1)S(1)} %get-tuple-element.24), channel_id=1, source_target_pairs={{0,96},{32,64},{64,32},{96,0},{1,97},{33,65},{65,33},{97,1},{2,98}... | collective-permute-start | bytes 98312 | tf_op jit(solution)/shard_map/ppermute | solution.py:332
  64.8 0.0 collective-permute-start.8
  64.8 1.4 %collective-permute-start.9 = (bf16[16,1024]{1,0:T(8,128)(2,1)S(1)}, bf16[16,1024]{1,0:T(8,128)(2,1)S(1)}, u32[]{:S(2)}, u32[]{:S(2)}) collective-permute-start(bf16[16,1024]{1,0:T(8,128)(2,1)S(1)} %get-tuple-element.23), channel_id=1, source_target_pairs={{0,64},{32,96},{64,0},{96,32},{1,65},{33,97},{65,1},{97,33},{2,66}... | collective-permute-start | bytes 98312 | tf_op jit(solution)/shard_map/ppermute | solution.py:332
  66.3 0.2 collective-permute-done.10.refs_3_
  66.4 0.0 collective-permute-done.8.refs_1_
  66.4 2.7 %collective-permute-done.9.refs_2_ = bf16[16,1024]{1,0:T(8,128)(2,1)S(1)} collective-permute-done((bf16[16,1024]{1,0:T(8,128)(2,1)S(1)}, bf16[16,1024]{1,0:T(8,128)(2,1)S(1)}, u32[]{:S(2)}, u32[]{:S(2)}) %collective-permute-start.9) | collective-permute-done | bytes 32800 | tf_op jit(solution)/shard_map/ppermute | solution.py:332
  69.1 0.7 %join_groups.1 = f32[16,4096]{1,0:T(8,128)} custom-call(s32[1]{0:T(128)} %bitcast.off_ref, f32[16,1024]{1,0:T(8,128)S(1)} %get-tuple-element.21.refs_0_, bf16[16,1024]{1,0:T(8,128)(2,1)S(1)} %collective-permute-done.8.refs_1_, bf16[16,1024]{1,0:T(8,128)(2,1)S(1)} %collective-permute-done.9.refs_2_, bf16[16,1024]{1,0:T(8,128)(2,1)S(1)} %collective-permute-done.10.refs_3_), custom_call_target="tpu_custom_call" | custom-call | tf_op jit(solution)/shard_map/join_groups/pallas_call | solution.py:335
  (1 shorter events, 0.0 us)
Async XLA Ops:
  0.0 43.1 %copy-start = (bf16[32,128,128]{2,1,0:T(8,128)(2,1)S(1)}, bf16[32,128,128]{2,1,0:T(8,128)(2,1)}, u32[]{:S(2)}) copy-start(bf16[32,128,128]{2,1,0:T(8,128)(2,1)} %param.11) | copy-start | bytes 3145732
  1.7 21.6 %collective-permute-start = (bf16[33,32,128]{2,1,0:T(8,128)(2,1)S(1)}, bf16[33,32,128]{2,1,0:T(8,128)(2,1)S(1)}, u32[]{:S(2)}, u32[]{:S(2)}) collective-permute-start(bf16[33,32,128]{2,1,0:T(8,128)(2,1)S(1)} %get-tuple-element.15.refs_0_), channel_id=1, source_target_pairs={{0,1},{1,64},{64,65},{65,0},{2,3},{3,66},{66,67},{67,2},{4,5},{5,6... | collective-permute-start | bytes 811016 | tf_op jit(solution)/shard_map/ppermute | solution.py:276
  4.3 19.0 %collective-permute-start.1 = (bf16[33,32,128]{2,1,0:T(8,128)(2,1)S(1)}, bf16[33,32,128]{2,1,0:T(8,128)(2,1)S(1)}, u32[]{:S(2)}, u32[]{:S(2)}) collective-permute-start(bf16[33,32,128]{2,1,0:T(8,128)(2,1)S(1)} %get-tuple-element.15.refs_0_), channel_id=1, source_target_pairs={{0,65},{1,0},{64,1},{65,64},{2,67},{3,2},{66,3},{67,66},{4,69},{5,... | collective-permute-start | bytes 811016 | tf_op jit(solution)/shard_map/ppermute | solution.py:276
  6.5 16.9 %collective-permute-start.2 = (bf16[33,32,128]{2,1,0:T(8,128)(2,1)S(1)}, bf16[33,32,128]{2,1,0:T(8,128)(2,1)S(1)}, u32[]{:S(2)}, u32[]{:S(2)}) collective-permute-start(bf16[33,32,128]{2,1,0:T(8,128)(2,1)S(1)} %get-tuple-element.15.refs_0_), channel_id=1, source_target_pairs={{0,64},{1,65},{64,0},{65,1},{2,66},{3,67},{66,2},{67,3},{4,68},{5,... | collective-permute-start | bytes 811016 | tf_op jit(solution)/shard_map/ppermute | solution.py:276
  7.7 15.6 %all-to-all-start = ((s32[32,2,128]{2,1,0:T(2,128)}), s32[32,2,128]{2,1,0:T(2,128)S(1)}, u32[]{:S(2)}, u32[]{:S(2)}) async-start(s32[32,2,128]{2,1,0:T(2,128)} %bitcast.18), calls=%async_computation | async-start | bytes 65536 | tf_op jit(solution)/shard_map/all_to_all | solution.py:278
  16.3 9.7 %collective-permute-start.4 = (bf16[33,32,128]{2,1,0:T(8,128)(2,1)S(1)}, bf16[33,32,128]{2,1,0:T(8,128)(2,1)S(1)}, u32[]{:S(2)}, u32[]{:S(2)}) collective-permute-start(bf16[33,32,128]{2,1,0:T(8,128)(2,1)S(1)} %get-tuple-element.15.refs_0_), channel_id=1, source_target_pairs={{0,32},{32,0},{1,33},{33,1},{2,34},{34,2},{3,35},{35,3},{4,36},{36... | collective-permute-start | bytes 811016 | tf_op jit(solution)/shard_map/ppermute | solution.py:282
  23.3 2.7 %collective-permute-start.5 = (bf16[33,32,128]{2,1,0:T(8,128)(2,1)S(1)}, bf16[33,32,128]{2,1,0:T(8,128)(2,1)S(1)}, u32[]{:S(2)}, u32[]{:S(2)}) collective-permute-start(bf16[33,32,128]{2,1,0:T(8,128)(2,1)S(1)} %collective-permute-done.refs_1_), channel_id=1, source_target_pairs={{0,32},{32,0},{1,33},{33,1},{2,34},{34,2},{3,35},{35,3},{4,36},{36... | collective-permute-start | bytes 811016 | tf_op jit(solution)/shard_map/ppermute | solution.py:282
  24.0 2.0 %collective-permute-start.6 = (bf16[33,32,128]{2,1,0:T(8,128)(2,1)S(1)}, bf16[33,32,128]{2,1,0:T(8,128)(2,1)S(1)}, u32[]{:S(2)}, u32[]{:S(2)}) collective-permute-start(bf16[33,32,128]{2,1,0:T(8,128)(2,1)S(1)} %collective-permute-done.1.refs_2_), channel_id=1, source_target_pairs={{0,32},{32,0},{1,33},{33,1},{2,34},{34,2},{3,35},{35,3},{4,36},{36... | collective-permute-start | bytes 811016 | tf_op jit(solution)/shard_map/ppermute | solution.py:282
  24.1 1.9 %collective-permute-start.7 = (bf16[33,32,128]{2,1,0:T(8,128)(2,1)S(1)}, bf16[33,32,128]{2,1,0:T(8,128)(2,1)S(1)}, u32[]{:S(2)}, u32[]{:S(2)}) collective-permute-start(bf16[33,32,128]{2,1,0:T(8,128)(2,1)S(1)} %collective-permute-done.2.refs_3_), channel_id=1, source_target_pairs={{0,32},{32,0},{1,33},{33,1},{2,34},{34,2},{3,35},{35,3},{4,36},{36... | collective-permute-start | bytes 811016 | tf_op jit(solution)/shard_map/ppermute | solution.py:282
  24.5 4.3 %collective-permute-start.3 = (s32[64,128]{1,0:T(8,128)S(1)}, s32[64,128]{1,0:T(8,128)S(1)}, u32[]{:S(2)}, u32[]{:S(2)}) collective-permute-start(s32[64,128]{1,0:T(8,128)S(1)} %bitcast.14), channel_id=1, source_target_pairs={{0,64},{64,0},{1,65},{65,1},{2,66},{66,2},{3,67},{67,3},{4,68},{68... | collective-permute-start | bytes 98312 | tf_op jit(solution)/shard_map/ppermute | solution.py:283
  39.5 18.9 %all-to-all-start.1 = ((bf16[16,8,8,512]{3,2,1,0:T(8,128)(2,1)}), bf16[16,8,8,512]{3,2,1,0:T(8,128)(2,1)S(1)}, u32[]{:S(2)}, u32[]{:S(2)}) async-start(bf16[16,8,8,512]{3,2,1,0:T(8,128)(2,1)} %stack_windows.1), calls=%async_computation.1 | async-start | bytes 2097152 | tf_op jit(solution)/shard_map/all_to_all | solution.py:317
  60.2 6.3 %collective-permute-start.10 = (bf16[16,1024]{1,0:T(8,128)(2,1)S(1)}, bf16[16,1024]{1,0:T(8,128)(2,1)S(1)}, u32[]{:S(2)}, u32[]{:S(2)}) collective-permute-start(bf16[16,1024]{1,0:T(8,128)(2,1)S(1)} %get-tuple-element.24), channel_id=1, source_target_pairs={{0,96},{32,64},{64,32},{96,0},{1,97},{33,65},{65,33},{97,1},{2,98}... | collective-permute-start | bytes 98312 | tf_op jit(solution)/shard_map/ppermute | solution.py:332
  64.8 1.6 %collective-permute-start.8 = (bf16[16,1024]{1,0:T(8,128)(2,1)S(1)}, bf16[16,1024]{1,0:T(8,128)(2,1)S(1)}, u32[]{:S(2)}, u32[]{:S(2)}) collective-permute-start(bf16[16,1024]{1,0:T(8,128)(2,1)S(1)} %get-tuple-element.22), channel_id=1, source_target_pairs={{0,32},{32,0},{64,96},{96,64},{1,33},{33,1},{65,97},{97,65},{2,34}... | collective-permute-start | bytes 98312 | tf_op jit(solution)/shard_map/ppermute | solution.py:332
  64.8 4.3 %collective-permute-start.9 = (bf16[16,1024]{1,0:T(8,128)(2,1)S(1)}, bf16[16,1024]{1,0:T(8,128)(2,1)S(1)}, u32[]{:S(2)}, u32[]{:S(2)}) collective-permute-start(bf16[16,1024]{1,0:T(8,128)(2,1)S(1)} %get-tuple-element.23), channel_id=1, source_target_pairs={{0,64},{32,96},{64,0},{96,32},{1,65},{33,97},{65,1},{97,33},{2,66}... | collective-permute-start | bytes 98312 | tf_op jit(solution)/shard_map/ppermute | solution.py:332

commit v4 on v3

--- a/solution.py
+++ b/solution.py
@@ -224,7 +224,7 @@
 
 def join_kernel(off_ref, *refs):
     out_ref = refs[-1]
-    for apart, ref in enumerate(refs[:-1]):
+    for apart, ref in zip((0, 2, 3, 1), refs[:-1]):
         width = ref.shape[1]
         start = pl.multiple_of((off_ref[0] ^ apart) * width, LANES)
         out_ref[:, pl.ds(start, width)] = ref[...].astype(out_ref.dtype)
@@ -338,7 +338,7 @@
         in_specs=[smem] + [vmem] * 4,
         out_specs=vmem,
         name="join_groups",
-    )(off.reshape(1), *map(in_vmem, (own, beside, far, across)))
+    )(off.reshape(1), *map(in_vmem, (own, far, across, beside)))
 
 
 def solution(mesh):

time: 70.7 us -> 72.4 us (1.024); the launches traced: 69.8 us -> 72.7 us
  Pallas kernels: 16.7 us -> 18.9 us
    pallas_call x1, Pallas kernels: 10.6 us -> 12.8 us  [local(): pl.pallas_call(functools.partial(stack_kernel, blocks=blocks, chunks=chun...]
where the time goes in v4:
time: 72.4 us; the launch traced here: 72.7 us
  starting transfers between devices  27.7 us (38%)
  waiting for transfers between devices  25 us (35%)
  Pallas kernels  18.9 us (26%)
  local copies, waits for them, and re-layouts  1.12 us (2%)
    all_to_all x1, waiting for transfers between devices, local(): arrived = lax.all_to_all(stacked, PLANE, 0, 0, tiled=True)  14.1 us
    pallas_call x1, Pallas kernels, local(): pl.pallas_call(functools.partial(stack_kernel, blocks=blocks, chunks=chun...  12.8 us
    all_to_all x1, starting transfers between devices, local(): meta = lax.all_to_all(row, ('core',) + PLANE, 0, 0, tiled=True)  8.6 us
    all_to_all x1, waiting for transfers between devices, local(): meta = lax.all_to_all(row, ('core',) + PLANE, 0, 0, tiled=True)  6.69 us
    ppermute x3, starting transfers between devices, local(): lax.ppermute(strip, OFF, [(index, index ^ apart) for index in range(offs)])  6.45 us
    ppermute x3, starting transfers between devices, local(): lax.ppermute(sent, ('zh', 'zl'), ring_pairs(step))  5.96 us
    all_to_all x1, starting transfers between devices, local(): arrived = lax.all_to_all(stacked, PLANE, 0, 0, tiled=True)  3.66 us
    ppermute x3, waiting for transfers between devices, local(): lax.ppermute(strip, OFF, [(index, index ^ apart) for index in range(offs)])  3.21 us
  transfers between devices with their start and end apart: 13, of which 5 were waited for; matrix products, arithmetic and copies ran while one was open for 2% of the time, Pallas kernels for 3%

profile of v4, /device:TPU:1, one launch (start us, length us, event | category | flops | bytes accessed | tf_op | source)
XLA Modules:
  0.0 72.7 jit_solution(385267389227389446)
XLA Ops:
  0.0 0.0 copy-start
  0.0 1.7 %prepare_traces.1 = (bf16[33,32,128]{2,1,0:T(8,128)(2,1)S(1)}, s32[64,128]{1,0:T(8,128)}) custom-call(s32[1]{0:T(128)} %bitcast.off_ref, bf16[32,4096]{1,0:T(8,128)(2,1)} %bitcast.17, s32[4,8]{1,0:T(4,128)} %bitcast.19, s32[8,32]{1,0:T(8,128)} %refs_2_.1, s32[1,8]{1,0:T(1,128)} %bitcast.20), custom_call_target="tpu_custom_call" | custom-call | tf_op jit(solution)/shard_map/prepare_traces/pallas_call | solution.py:256
  1.7 2.5 %collective-permute-start = (bf16[33,32,128]{2,1,0:T(8,128)(2,1)S(1)}, bf16[33,32,128]{2,1,0:T(8,128)(2,1)S(1)}, u32[]{:S(2)}, u32[]{:S(2)}) collective-permute-start(bf16[33,32,128]{2,1,0:T(8,128)(2,1)S(1)} %get-tuple-element.15.refs_0_), channel_id=1, source_target_pairs={{0,1},{1,64},{64,65},{65,0},{2,3},{3,66},{66,67},{67,2},{4,5},{5,6... | collective-permute-start | bytes 811016 | tf_op jit(solution)/shard_map/ppermute | solution.py:276
  4.3 2.2 %collective-permute-start.1 = (bf16[33,32,128]{2,1,0:T(8,128)(2,1)S(1)}, bf16[33,32,128]{2,1,0:T(8,128)(2,1)S(1)}, u32[]{:S(2)}, u32[]{:S(2)}) collective-permute-start(bf16[33,32,128]{2,1,0:T(8,128)(2,1)S(1)} %get-tuple-element.15.refs_0_), channel_id=1, source_target_pairs={{0,65},{1,0},{64,1},{65,64},{2,67},{3,2},{66,3},{67,66},{4,69},{5,... | collective-permute-start | bytes 811016 | tf_op jit(solution)/shard_map/ppermute | solution.py:276
  6.5 1.2 %collective-permute-start.2 = (bf16[33,32,128]{2,1,0:T(8,128)(2,1)S(1)}, bf16[33,32,128]{2,1,0:T(8,128)(2,1)S(1)}, u32[]{:S(2)}, u32[]{:S(2)}) collective-permute-start(bf16[33,32,128]{2,1,0:T(8,128)(2,1)S(1)} %get-tuple-element.15.refs_0_), channel_id=1, source_target_pairs={{0,64},{1,65},{64,0},{65,1},{2,66},{3,67},{66,2},{67,3},{4,68},{5,... | collective-permute-start | bytes 811016 | tf_op jit(solution)/shard_map/ppermute | solution.py:276
  7.7 8.6 %all-to-all-start = ((s32[32,2,128]{2,1,0:T(2,128)}), s32[32,2,128]{2,1,0:T(2,128)S(1)}, u32[]{:S(2)}, u32[]{:S(2)}) async-start(s32[32,2,128]{2,1,0:T(2,128)} %bitcast.18), calls=%async_computation | async-start | bytes 65536 | tf_op jit(solution)/shard_map/all_to_all | solution.py:278
  16.3 0.3 collective-permute-start.4
  16.6 6.7 %all-to-all-done = s32[32,2,128]{2,1,0:T(2,128)S(1)} async-done(((s32[32,2,128]{2,1,0:T(2,128)}), s32[32,2,128]{2,1,0:T(2,128)S(1)}, u32[]{:S(2)}, u32[]{:S(2)}) %all-to-all-start) | async-done | bytes 32800 | tf_op jit(solution)/shard_map/all_to_all | solution.py:278
  23.3 0.0 collective-permute-done.refs_1_
  23.3 0.0 collective-permute-done.1.refs_2_
  23.3 0.0 collective-permute-done.2.refs_3_
  23.3 0.7 collective-permute-start.5
  24.0 0.1 collective-permute-start.6
  24.1 0.4 collective-permute-start.7
  24.5 1.5 %collective-permute-start.3 = (s32[64,128]{1,0:T(8,128)S(1)}, s32[64,128]{1,0:T(8,128)S(1)}, u32[]{:S(2)}, u32[]{:S(2)}) collective-permute-start(s32[64,128]{1,0:T(8,128)S(1)} %bitcast.14), channel_id=1, source_target_pairs={{0,64},{64,0},{1,65},{65,1},{2,66},{66,2},{3,67},{67,3},{4,68},{68... | collective-permute-start | bytes 98312 | tf_op jit(solution)/shard_map/ppermute | solution.py:283
  26.0 0.0 collective-permute-done.4.refs_4_
  26.0 0.0 collective-permute-done.5.refs_5_
  26.0 0.0 collective-permute-done.6.refs_6_
  26.0 0.0 collective-permute-done.7.refs_7_
  26.0 1.8 %place_traces.1.pairs_ref = bf16[1023,16,128]{2,1,0:T(8,128)(2,1)S(1)} custom-call(s32[1]{0:T(128)} %bitcast.1.z_ref, s32[1]{0:T(128)} %bitcast.10.core_ref, bf16[33,32,128]{2,1,0:T(8,128)(2,1)S(1)} %get-tuple-element.15.refs_0_, bf16[33,32,128]{2,1,0:T(8,128)(2,1)S(1)} %collective-permute-done.refs_1_, ...), custom_call_target="tpu_custom_call" | custom-call | tf_op jit(solution)/shard_map/place_traces/pallas_call | solution.py:284
  27.9 0.9 %collective-permute-done.3 = s32[64,128]{1,0:T(8,128)S(1)} collective-permute-done((s32[64,128]{1,0:T(8,128)S(1)}, s32[64,128]{1,0:T(8,128)S(1)}, u32[]{:S(2)}, u32[]{:S(2)}) %collective-permute-start.3) | collective-permute-done | bytes 32800 | tf_op jit(solution)/shard_map/ppermute | solution.py:283
  28.8 12.8 %stack_windows.1 = bf16[16,8,8,512]{3,2,1,0:T(8,128)(2,1)} custom-call(s32[1]{0:T(128)} %bitcast.1.z_ref, s32[8192]{0:T(1024)S(1)} %bitcast.15, s32[8192]{0:T(1024)S(1)} %bitcast.16, bf16[1023,16,128]{2,1,0:T(8,128)(2,1)S(1)} %place_traces.1.pairs_ref), custom_call_target="tpu_custom_call" | custom-call | tf_op jit(solution)/shard_map/stack_windows/pallas_call | solution.py:301
  41.6 3.7 %all-to-all-start.1 = ((bf16[16,8,8,512]{3,2,1,0:T(8,128)(2,1)}), bf16[16,8,8,512]{3,2,1,0:T(8,128)(2,1)S(1)}, u32[]{:S(2)}, u32[]{:S(2)}) async-start(bf16[16,8,8,512]{3,2,1,0:T(8,128)(2,1)} %stack_windows.1), calls=%async_computation.1 | async-start | bytes 2097152 | tf_op jit(solution)/shard_map/all_to_all | solution.py:317
  45.3 0.0 copy-done
  45.3 1.1 %dynamic-slice_bitcast_fusion.interp_ref = bf16[8,64,512]{2,1,0:T(8,128)(2,1)S(1)} fusion(bf16[32,512,64]{1,2,0:T(8,128)(2,1)} %param.10, s32[]{:T(128)S(6)} %select_n.4), kind=kLoop, calls=%fused_computation | loop fusion | bytes 1048580 | tf_op jit(solution)/shard_map/dynamic_slice | solution.py:319
  46.4 14.1 %all-to-all-done.1.stacked_ref = bf16[16,8,8,512]{3,2,1,0:T(8,128)(2,1)S(1)} async-done(((bf16[16,8,8,512]{3,2,1,0:T(8,128)(2,1)}), bf16[16,8,8,512]{3,2,1,0:T(8,128)(2,1)S(1)}, u32[]{:S(2)}, u32[]{:S(2)}) %all-to-all-start.1) | async-done | bytes 1048608 | tf_op jit(solution)/shard_map/all_to_all | solution.py:317
  60.5 1.8 %image_groups.1 = (f32[16,1024]{1,0:T(8,128)S(1)}, bf16[16,1024]{1,0:T(8,128)(2,1)S(1)}, bf16[16,1024]{1,0:T(8,128)(2,1)S(1)}, bf16[16,1024]{1,0:T(8,128)(2,1)S(1)}) custom-call(s32[1]{0:T(128)} %bitcast.off_ref, bf16[16,8,8,512]{3,2,1,0:T(8,128)(2,1)S(1)} %all-to-all-done.1.stacked_ref, bf16[8,64,512]{2,1,0:T(8,128)(2,1)S(1)} %dynamic-slice_bitcast_fusion.interp_ref, ...), custom_call_target="tpu_custom_call" | custom-call | tf_op jit(solution)/shard_map/image_groups/pallas_call | solution.py:322
  62.3 3.2 %collective-permute-start.10 = (bf16[16,1024]{1,0:T(8,128)(2,1)S(1)}, bf16[16,1024]{1,0:T(8,128)(2,1)S(1)}, u32[]{:S(2)}, u32[]{:S(2)}) collective-permute-start(bf16[16,1024]{1,0:T(8,128)(2,1)S(1)} %get-tuple-element.24), channel_id=1, source_target_pairs={{0,32},{32,0},{64,96},{96,64},{1,33},{33,1},{65,97},{97,65},{2,34}... | collective-permute-start | bytes 98312 | tf_op jit(solution)/shard_map/ppermute | solution.py:332
  65.5 1.6 %collective-permute-start.8 = (bf16[16,1024]{1,0:T(8,128)(2,1)S(1)}, bf16[16,1024]{1,0:T(8,128)(2,1)S(1)}, u32[]{:S(2)}, u32[]{:S(2)}) collective-permute-start(bf16[16,1024]{1,0:T(8,128)(2,1)S(1)} %get-tuple-element.22), channel_id=1, source_target_pairs={{0,64},{32,96},{64,0},{96,32},{1,65},{33,97},{65,1},{97,33},{2,66}... | collective-permute-start | bytes 98312 | tf_op jit(solution)/shard_map/ppermute | solution.py:332
  67.1 1.7 %collective-permute-start.9 = (bf16[16,1024]{1,0:T(8,128)(2,1)S(1)}, bf16[16,1024]{1,0:T(8,128)(2,1)S(1)}, u32[]{:S(2)}, u32[]{:S(2)}) collective-permute-start(bf16[16,1024]{1,0:T(8,128)(2,1)S(1)} %get-tuple-element.23), channel_id=1, source_target_pairs={{0,96},{32,64},{64,32},{96,0},{1,97},{33,65},{65,33},{97,1},{2,98}... | collective-permute-start | bytes 98312 | tf_op jit(solution)/shard_map/ppermute | solution.py:332
  68.8 0.0 collective-permute-done.10.refs_3_
  68.8 1.1 %collective-permute-done.8.refs_1_ = bf16[16,1024]{1,0:T(8,128)(2,1)S(1)} collective-permute-done((bf16[16,1024]{1,0:T(8,128)(2,1)S(1)}, bf16[16,1024]{1,0:T(8,128)(2,1)S(1)}, u32[]{:S(2)}, u32[]{:S(2)}) %collective-permute-start.8) | collective-permute-done | bytes 32800 | tf_op jit(solution)/shard_map/ppermute | solution.py:332
  69.8 2.2 %collective-permute-done.9.refs_2_ = bf16[16,1024]{1,0:T(8,128)(2,1)S(1)} collective-permute-done((bf16[16,1024]{1,0:T(8,128)(2,1)S(1)}, bf16[16,1024]{1,0:T(8,128)(2,1)S(1)}, u32[]{:S(2)}, u32[]{:S(2)}) %collective-permute-start.9) | collective-permute-done | bytes 32800 | tf_op jit(solution)/shard_map/ppermute | solution.py:332
  72.0 0.7 join_groups.1
  (1 shorter events, 0.0 us)
Async XLA Ops:
  0.0 45.3 %copy-start = (bf16[32,128,128]{2,1,0:T(8,128)(2,1)S(1)}, bf16[32,128,128]{2,1,0:T(8,128)(2,1)}, u32[]{:S(2)}) copy-start(bf16[32,128,128]{2,1,0:T(8,128)(2,1)} %param.11) | copy-start | bytes 3145732
  1.7 21.6 %collective-permute-start = (bf16[33,32,128]{2,1,0:T(8,128)(2,1)S(1)}, bf16[33,32,128]{2,1,0:T(8,128)(2,1)S(1)}, u32[]{:S(2)}, u32[]{:S(2)}) collective-permute-start(bf16[33,32,128]{2,1,0:T(8,128)(2,1)S(1)} %get-tuple-element.15.refs_0_), channel_id=1, source_target_pairs={{0,1},{1,64},{64,65},{65,0},{2,3},{3,66},{66,67},{67,2},{4,5},{5,6... | collective-permute-start | bytes 811016 | tf_op jit(solution)/shard_map/ppermute | solution.py:276
  4.3 19.0 %collective-permute-start.1 = (bf16[33,32,128]{2,1,0:T(8,128)(2,1)S(1)}, bf16[33,32,128]{2,1,0:T(8,128)(2,1)S(1)}, u32[]{:S(2)}, u32[]{:S(2)}) collective-permute-start(bf16[33,32,128]{2,1,0:T(8,128)(2,1)S(1)} %get-tuple-element.15.refs_0_), channel_id=1, source_target_pairs={{0,65},{1,0},{64,1},{65,64},{2,67},{3,2},{66,3},{67,66},{4,69},{5,... | collective-permute-start | bytes 811016 | tf_op jit(solution)/shard_map/ppermute | solution.py:276
  6.5 16.9 %collective-permute-start.2 = (bf16[33,32,128]{2,1,0:T(8,128)(2,1)S(1)}, bf16[33,32,128]{2,1,0:T(8,128)(2,1)S(1)}, u32[]{:S(2)}, u32[]{:S(2)}) collective-permute-start(bf16[33,32,128]{2,1,0:T(8,128)(2,1)S(1)} %get-tuple-element.15.refs_0_), channel_id=1, source_target_pairs={{0,64},{1,65},{64,0},{65,1},{2,66},{3,67},{66,2},{67,3},{4,68},{5,... | collective-permute-start | bytes 811016 | tf_op jit(solution)/shard_map/ppermute | solution.py:276
  7.7 15.6 %all-to-all-start = ((s32[32,2,128]{2,1,0:T(2,128)}), s32[32,2,128]{2,1,0:T(2,128)S(1)}, u32[]{:S(2)}, u32[]{:S(2)}) async-start(s32[32,2,128]{2,1,0:T(2,128)} %bitcast.18), calls=%async_computation | async-start | bytes 65536 | tf_op jit(solution)/shard_map/all_to_all | solution.py:278
  16.3 9.7 %collective-permute-start.4 = (bf16[33,32,128]{2,1,0:T(8,128)(2,1)S(1)}, bf16[33,32,128]{2,1,0:T(8,128)(2,1)S(1)}, u32[]{:S(2)}, u32[]{:S(2)}) collective-permute-start(bf16[33,32,128]{2,1,0:T(8,128)(2,1)S(1)} %get-tuple-element.15.refs_0_), channel_id=1, source_target_pairs={{0,32},{32,0},{1,33},{33,1},{2,34},{34,2},{3,35},{35,3},{4,36},{36... | collective-permute-start | bytes 811016 | tf_op jit(solution)/shard_map/ppermute | solution.py:282
  23.3 2.7 %collective-permute-start.5 = (bf16[33,32,128]{2,1,0:T(8,128)(2,1)S(1)}, bf16[33,32,128]{2,1,0:T(8,128)(2,1)S(1)}, u32[]{:S(2)}, u32[]{:S(2)}) collective-permute-start(bf16[33,32,128]{2,1,0:T(8,128)(2,1)S(1)} %collective-permute-done.refs_1_), channel_id=1, source_target_pairs={{0,32},{32,0},{1,33},{33,1},{2,34},{34,2},{3,35},{35,3},{4,36},{36... | collective-permute-start | bytes 811016 | tf_op jit(solution)/shard_map/ppermute | solution.py:282
  24.0 2.0 %collective-permute-start.6 = (bf16[33,32,128]{2,1,0:T(8,128)(2,1)S(1)}, bf16[33,32,128]{2,1,0:T(8,128)(2,1)S(1)}, u32[]{:S(2)}, u32[]{:S(2)}) collective-permute-start(bf16[33,32,128]{2,1,0:T(8,128)(2,1)S(1)} %collective-permute-done.1.refs_2_), channel_id=1, source_target_pairs={{0,32},{32,0},{1,33},{33,1},{2,34},{34,2},{3,35},{35,3},{4,36},{36... | collective-permute-start | bytes 811016 | tf_op jit(solution)/shard_map/ppermute | solution.py:282
  24.1 1.9 %collective-permute-start.7 = (bf16[33,32,128]{2,1,0:T(8,128)(2,1)S(1)}, bf16[33,32,128]{2,1,0:T(8,128)(2,1)S(1)}, u32[]{:S(2)}, u32[]{:S(2)}) collective-permute-start(bf16[33,32,128]{2,1,0:T(8,128)(2,1)S(1)} %collective-permute-done.2.refs_3_), channel_id=1, source_target_pairs={{0,32},{32,0},{1,33},{33,1},{2,34},{34,2},{3,35},{35,3},{4,36},{36... | collective-permute-start | bytes 811016 | tf_op jit(solution)/shard_map/ppermute | solution.py:282
  24.5 4.3 %collective-permute-start.3 = (s32[64,128]{1,0:T(8,128)S(1)}, s32[64,128]{1,0:T(8,128)S(1)}, u32[]{:S(2)}, u32[]{:S(2)}) collective-permute-start(s32[64,128]{1,0:T(8,128)S(1)} %bitcast.14), channel_id=1, source_target_pairs={{0,64},{64,0},{1,65},{65,1},{2,66},{66,2},{3,67},{67,3},{4,68},{68... | collective-permute-start | bytes 98312 | tf_op jit(solution)/shard_map/ppermute | solution.py:283
  41.6 18.9 %all-to-all-start.1 = ((bf16[16,8,8,512]{3,2,1,0:T(8,128)(2,1)}), bf16[16,8,8,512]{3,2,1,0:T(8,128)(2,1)S(1)}, u32[]{:S(2)}, u32[]{:S(2)}) async-start(bf16[16,8,8,512]{3,2,1,0:T(8,128)(2,1)} %stack_windows.1), calls=%async_computation.1 | async-start | bytes 2097152 | tf_op jit(solution)/shard_map/all_to_all | solution.py:317
  62.3 6.5 %collective-permute-start.10 = (bf16[16,1024]{1,0:T(8,128)(2,1)S(1)}, bf16[16,1024]{1,0:T(8,128)(2,1)S(1)}, u32[]{:S(2)}, u32[]{:S(2)}) collective-permute-start(bf16[16,1024]{1,0:T(8,128)(2,1)S(1)} %get-tuple-element.24), channel_id=1, source_target_pairs={{0,32},{32,0},{64,96},{96,64},{1,33},{33,1},{65,97},{97,65},{2,34}... | collective-permute-start | bytes 98312 | tf_op jit(solution)/shard_map/ppermute | solution.py:332
  65.5 4.3 %collective-permute-start.8 = (bf16[16,1024]{1,0:T(8,128)(2,1)S(1)}, bf16[16,1024]{1,0:T(8,128)(2,1)S(1)}, u32[]{:S(2)}, u32[]{:S(2)}) collective-permute-start(bf16[16,1024]{1,0:T(8,128)(2,1)S(1)} %get-tuple-element.22), channel_id=1, source_target_pairs={{0,64},{32,96},{64,0},{96,32},{1,65},{33,97},{65,1},{97,33},{2,66}... | collective-permute-start | bytes 98312 | tf_op jit(solution)/shard_map/ppermute | solution.py:332
  67.1 4.9 %collective-permute-start.9 = (bf16[16,1024]{1,0:T(8,128)(2,1)S(1)}, bf16[16,1024]{1,0:T(8,128)(2,1)S(1)}, u32[]{:S(2)}, u32[]{:S(2)}) collective-permute-start(bf16[16,1024]{1,0:T(8,128)(2,1)S(1)} %get-tuple-element.23), channel_id=1, source_target_pairs={{0,96},{32,64},{64,32},{96,0},{1,97},{33,65},{65,33},{97,1},{2,98}... | collective-permute-start | bytes 98312 | tf_op jit(solution)/shard_map/ppermute | solution.py:332
